TPU v7x, 128 devices: a whole 4x4x4 slice. The times are simulated.
128 devices in a mesh: tp: 8 (over y, x_lo), lat: 16 (over x_hi, z, core).
Axes of the slice: x: 4 (x_hi: 2, x_lo: 2; x = x_hi * 2 + x_lo), y: 4, z: 4, core: 2. Of those that a mesh axis runs over, the one named last changes fastest.
Arguments:
- attn_out: bfloat16 [2048, 4096], P('lat', 'tp'), may hold values from -6 to 6
- w_out: bfloat16 [4096, 8192], P('tp'), may hold values from -0.09375 to 0.09375
- resid_in: bfloat16 [2048, 8192], P(('lat', 'tp')), may hold values from -6 to 6
- positions: int32 [256], replicated, may hold values from 0 to 2047
- w_enc: bfloat16 [8192, 131072], P(None, ('tp', 'lat')), may hold values from -0.0625 to 0.0625
- b_enc: float32 [131072], P(('tp', 'lat')), may hold values from -3 to 3
- dec_norm: float32 [131072], P(('tp', 'lat')), may hold values from 0.05 to 0.5
- b_dec: float32 [8192], replicated, may hold values from -3 to 3
Outputs:
- stream: bfloat16 [2048, 8192], P(('lat', 'tp'))
- codes: bfloat16 [256, 131072], P(None, ('tp', 'lat'))
- recon: bfloat16 [256, 8192], P(('tp', 'lat'))
- error: float32 [256], P(('tp', 'lat'))
All inputs are finite; a program needn't handle non-finite values.
Results may differ from a plain program's by a relative error of at most 0.0059.
Values may be sent and summed in bfloat16 or wider, within the bound.
No kernel may reach another device: no remote copies, remote signals or barrier semaphores. Data moves between devices by JAX's collectives and lax.ppermute only.
A program may use at most 128 MiB of HBM per device.

v0:
```python
import jax
import jax.numpy as jnp
from jax import lax
from jax.experimental import pallas as pl
from jax.experimental.pallas import tpu as pltpu
from jax.sharding import Mesh, PartitionSpec as P


AXES = ("y", "xl", "xh", "z", "c")
SIZES = (4, 2, 2, 4, 2)
TP = ("y", "xl")
LAT = ("xh", "z", "c")
bf16 = jnp.bfloat16
f32 = jnp.float32


def _x(i):
    i %= 4
    return (i % 2) * 2 + i // 2


def shift(v, ax, s):
    if ax == "x":
        return lax.ppermute(v, ("xl", "xh"), [(_x(i), _x(i + s)) for i in range(4)])
    n = 4 if ax in "yz" else 2
    return lax.ppermute(v, ax, [(i, (i + s) % n) for i in range(n)])


def coord(ax):
    if ax == "x":
        return lax.axis_index("xh") * 2 + lax.axis_index("xl")
    return lax.axis_index(ax)


def cut(v, starts, sizes):
    return lax.dynamic_slice(v, starts, sizes, allow_negative_indices=False)


def take(v, i, axis=0):
    axis %= v.ndim
    sizes = [1 if a == axis else n for a, n in enumerate(v.shape)]
    return jnp.squeeze(cut(v, [i if a == axis else 0 for a in range(v.ndim)], sizes), axis)


def reduce_ring(v, ax):
    me = coord(ax)
    got = [shift(take(v, (me + s) & 3), ax, s) for s in (2, 1, 3)]
    total = take(v, me).astype(f32)
    for g in got:
        total = total + g.astype(f32)
    return total


def gather_ring(v, ax):
    got = {s: shift(v, ax, s) for s in (2, 1, 3)}
    return jnp.stack([v, got[1], got[2], got[3]])


def swap(v, ax, bit):
    if ax == "x":
        return lax.ppermute(v, ("xl", "xh"), [(_x(i), _x(i ^ bit)) for i in range(4)])
    return lax.ppermute(v, ax, [(i, i ^ bit) for i in range(4)])


def gather_double(v, ax):
    two = jnp.stack([v, swap(v, ax, 1)])
    return jnp.concatenate([two, swap(two, ax, 2)])


def reduce_double(v, ax, bits):
    v = v.reshape((2, 2) + v.shape[1:])
    for bit, axis, (mine, other) in ((1, 1, bits[0]), (2, 0, bits[1])):
        v = take(v, mine, axis) + swap(take(v, other, axis).astype(bf16), ax, bit).astype(f32)
    return v


VM = pl.BlockSpec(memory_space=pltpu.VMEM)
SM = pl.BlockSpec(memory_space=pltpu.SMEM)
HB = pl.BlockSpec(memory_space=pltpu.HBM)


def limit(mib):
    return pltpu.CompilerParams(vmem_limit_bytes=mib * 1024 * 1024)


def hbm(v):
    return pltpu.with_memory_space_constraint(v, pltpu.HBM)


def project(cols, attn, w_out, resid, counts, dtypes):
    rows, inner = attn.shape
    few = resid.shape[0]
    width, steps = 512, sum(counts)

    def kernel(cols_ref, attn_hbm, w_ref, r_hbm, *rest):
        outs, (attn_ref, r_ref, buf, sems) = rest[:-4], rest[-4:]

        def span(i):
            return pl.ds(pl.multiple_of(cols_ref[i] * width, width), width)

        small = [
            pltpu.make_async_copy(attn_hbm, attn_ref, sems.at[steps]),
            pltpu.make_async_copy(r_hbm, r_ref, sems.at[steps + 1]),
        ]
        copies = [pltpu.make_async_copy(w_ref.at[:, span(i)], buf.at[i], sems.at[i]) for i in range(steps)]
        for copy in small + copies:
            copy.start()
        at = lax.broadcasted_iota(jnp.int32, (rows, few), 0) - cols_ref[3 * steps] * few
        place = jnp.where(at == lax.broadcasted_iota(jnp.int32, (rows, few), 1), 1.0, 0.0).astype(bf16)
        for copy in small:
            copy.wait()
        slots = [(o, j) for o, n in zip(outs, counts) for j in range(n)]
        for i, (o, j) in enumerate(slots):
            copies[i].wait()
            acc = jnp.dot(attn_ref[...], buf[i], preferred_element_type=f32)
            acc = acc + jnp.dot(place, r_ref[:, span(i)], preferred_element_type=f32)
            o[j] = acc.astype(o.dtype)

    return pl.pallas_call(
        kernel,
        in_specs=[SM, HB, HB, HB],
        out_specs=[VM] * len(counts),
        out_shape=[jax.ShapeDtypeStruct((n, rows, width), d) for n, d in zip(counts, dtypes)],
        scratch_shapes=[
            pltpu.VMEM(attn.shape, bf16),
            pltpu.VMEM(resid.shape, bf16),
            pltpu.VMEM((steps, inner, width), bf16),
            pltpu.SemaphoreType.DMA((steps + 2,)),
        ],
        compiler_params=limit(12),
        name="project",
    )(cols, hbm(attn), hbm(w_out), hbm(resid))


def autoencode(table, skip, own_a, oth_a, own_b, oth_b, w_enc, b_dec, b_enc, dec_norm, back):
    half, width = own_a.shape[2:]
    d_model, lat = w_enc.shape
    n = d_model // width
    per = n // 2
    split = d_model // 2
    out_width = 512

    def kernel(table_ref, oa_ref, ta_ref, ob_ref, tb_ref, w_ref, bd_ref, be_ref, dn_ref, back_ref, codes_ref, *rest):
        outs, (buf, sems) = rest[:4], rest[4:]

        def span(j):
            return pl.ds(pl.multiple_of(table_ref[skip + j] * width, width), width)

        copies = [pltpu.make_async_copy(w_ref.at[span(j)], buf.at[span(j)], sems.at[j]) for j in range(n)]
        for copy in copies:
            copy.start()
        total = None
        for h, (o_ref, t_ref) in enumerate(((oa_ref, ta_ref), (ob_ref, tb_ref))):
            for j in range(h * per, (h + 1) * per):
                i, k = j // 4 % 4, j % 4
                lhs = jnp.concatenate([o_ref[i, k], t_ref[i, k]], axis=0)
                lhs = (lhs.astype(f32) - bd_ref[table_ref[skip + j]]).astype(bf16)
                copies[j].wait()
                term = jnp.dot(lhs, buf[span(j)], preferred_element_type=f32)
                total = term if total is None else total + term
        pre = total + be_ref[...]
        codes = (jnp.maximum(pre, 0.0) * dn_ref[...]).astype(bf16)
        codes_ref[...] = jnp.dot(back_ref[...], codes, preferred_element_type=f32).astype(bf16)
        for i in range(d_model // out_width):
            own_ref, oth_ref = outs[:2] if i * out_width < split else outs[2:]
            first = i * out_width % split
            to = slice(first, first + out_width)
            w = buf[i * out_width : (i + 1) * out_width]
            r = lax.dot_general(codes, w, (((1,), (1,)), ((), ())), preferred_element_type=f32)
            own_ref[:, to] = r[:half]
            oth_ref[:, to] = r[half:].astype(bf16)

    own_shape = jax.ShapeDtypeStruct((half, split), f32)
    oth_shape = jax.ShapeDtypeStruct((half, split), bf16)
    return pl.pallas_call(
        kernel,
        in_specs=[SM, VM, VM, VM, VM, HB, VM, VM, VM, VM],
        out_specs=[VM] * 5,
        out_shape=[jax.ShapeDtypeStruct((2 * half, lat), bf16), own_shape, oth_shape, own_shape, oth_shape],
        scratch_shapes=[pltpu.VMEM((d_model, lat), bf16), pltpu.SemaphoreType.DMA((n,))],
        compiler_params=limit(22),
        name="autoencode",
    )(table, own_a, oth_a, own_b, oth_b, hbm(w_enc), b_dec.reshape(-1, 1, width), b_enc[None], dec_norm[None], back)


def step(attn_out, w_out, resid_in, positions, w_enc, b_enc, dec_norm, b_dec):
    y, xl, xh, z, c = (lax.axis_index(a) for a in AXES)
    x = coord("x")
    t = y * 2 + xl
    lat = xh * 8 + z * 2 + c
    own_rows = resid_in.shape[0]
    rows = attn_out.shape[0]

    def block(dy, dx, h):
        yy, xx = (y + dy) & 3, xl ^ dx
        return 8 + xx * 4 + yy if h else yy * 2 + xx

    cols = [block(dy, 1, 0) for dy in range(4)] + [block(dy, dx, 1) for dy in (2, 1, 3) for dx in (0, 1)]
    cols += [block(dy, 0, 0) for dy in range(4)] + [block(0, dx, 1) for dx in (0, 1)]

    def unit(yy, xx, h):
        return 16 + (xx & 1) * 8 + yy * 2 + (xx >> 1) if h else yy * 4 + (xx & 1) * 2 + (xx >> 1)

    four = range(4)
    units = [unit((y - s) & 3, x ^ e, 0) for s in four for e in four]
    units += [unit(y ^ e, (x - s) & 3, 1) for s in four for e in four]
    first = (y * 4 + x) * 8 + z * 2
    later = [(i + s) & 3 for i in (x, y, z) for s in four] + [(y - s) & 3 for s in four]
    y_bits = tuple((b, b ^ 1) for b in (y & 1, y >> 1))
    later += [b for pair in y_bits for b in pair] + [c, c ^ 1, xh, xh ^ 1, xl, xl ^ 1, x, y, z, first]
    homes = [((y - yy) & 3) * 2 + (xl ^ xx) for yy in four for xx in (0, 1)]
    later += homes
    table = lax.optimization_barrier(jnp.stack(cols + units + [t] + later))
    a_send, b2, b1, b3, a_keep, b_keep = project(
        table, attn_out, w_out, resid_in, (4, 2, 2, 2, 4, 2), (bf16,) * 4 + (f32,) * 2
    )
    a_got = shift(a_send, "xl", 1)
    b_got = [shift(b2, "y", 2), shift(b1, "y", 1), shift(b3, "y", 3)]
    a_more = [shift((a_keep[s] + a_got[s].astype(f32)).astype(bf16), "y", s) for s in (2, 1, 3)]

    def b_part(dx):
        return b_keep[dx] + b_got[0][dx].astype(f32) + b_got[1][dx].astype(f32) + b_got[2][dx].astype(f32)

    b_more = shift(b_part(1).astype(bf16), "xl", 1)
    a_sum = a_keep[0] + a_got[0].astype(f32)
    for g in a_more:
        a_sum = a_sum + g.astype(f32)
    b_sum = b_part(0) + b_more.astype(f32)
    stream = jnp.concatenate([a_sum, b_sum], axis=1).astype(bf16)

    def by_core(v):
        return v.reshape(4, 2, 2, 4, 2, 2).transpose(4, 0, 2, 1, 3, 5).reshape(2, 128)

    pos2 = by_core(positions)
    ids = lat * rows + lax.iota(jnp.int32, rows)

    def hot(p):
        return (p[:, None] == ids[None, :]).astype(bf16)

    def pick(h, s):
        return jnp.dot(h, s, preferred_element_type=f32).astype(bf16)

    hot_own, hot_oth = hot(take(pos2, c)), hot(take(pos2, c ^ 1))
    parts = stream.reshape(rows, 2, 2, 256)
    cut_own, cut_oth = (take(parts, i, 2).reshape(rows, 512) for i in (xh, xh ^ 1))
    both = lax.ppermute(pick(hot_oth, cut_oth), ("xh", "c"), [(i, i ^ 3) for i in range(4)])
    other_h = shift(pick(hot_own, cut_oth), "xh", 1)
    other_c = shift(pick(hot_oth, cut_own), "c", 1)
    v = pick(hot_own, cut_own) + both + other_h + other_c
    got = [shift(v, "z", s) for s in (2, 1, 3)]
    v = v + got[0] + got[1] + got[2]
    s4 = stream.reshape(4, 2, own_rows, 1024)
    s_got = shift(take(s4, xl ^ 1, 1), "xl", 1)
    v, s_got = lax.optimization_barrier((v, s_got))
    v = v.reshape(rows, 2, 256)

    a = gather_double(v[:, 0], "x")
    b = gather_double(v[:, 1], "y")
    a = gather_ring(a, "y")
    b = gather_ring(b, "x")
    a_oth = shift(a, "c", 1)
    b_oth = shift(b, "c", 1)

    idx2 = by_core(lax.iota(jnp.int32, 256))
    where = jnp.concatenate([take(idx2, c), take(idx2, c ^ 1)])
    back = (lax.iota(jnp.int32, 256)[:, None] == where[None, :]).astype(bf16)
    codes_out, own_a, oth_a, own_b, oth_b = autoencode(
        table, len(cols), a, a_oth, b, b_oth, w_enc, b_dec, b_enc, dec_norm, back
    )
    got_a = shift(oth_a, "c", 1)
    got_b = shift(oth_b, "c", 1)

    h_a = (own_a + got_a.astype(f32)).astype(bf16).reshape(4, 4, 8, 4096)
    h_b = (own_b + got_b.astype(f32)).astype(bf16).reshape(4, 4, 8, 4096)
    r_a = reduce_ring(h_a, "y")
    r_b = reduce_ring(jnp.moveaxis(h_b, 1, 0), "x")
    r_a = reduce_double(r_a, "x", ((xl, xl ^ 1), (xh, xh ^ 1)))
    r_b = reduce_double(r_b, "y", y_bits)
    r = jnp.concatenate([r_a, r_b], axis=1).astype(bf16).reshape(4, 2, 8192)
    full = reduce_ring(r, "z") + b_dec

    a_s, b_s, _ = lax.optimization_barrier((a, b, own_b))
    s_own = take(s4, xl, 1)
    s_two = jnp.stack([s_own, s_got])
    s_rel = [take(s_two, y, 1)] + [shift(take(s_two, (y + s) & 3, 1), "y", s) for s in (1, 2, 3)]
    s_rel = jnp.stack(s_rel).reshape(8, own_rows, 1024)

    def home(yy, xx, h):
        return take(s_rel[:, :, h * 512 : (h + 1) * 512], homes[yy * 2 + xx])

    pieces = [home(yy, xx, 0) for yy in four for xx in (0, 1)]
    pieces += [home(yy, xx, 1) for xx in (0, 1) for yy in four]
    stream_out = jnp.concatenate(pieces, axis=1)

    mine_a, mine_b = (cut(v.reshape(16, 128, 256), (0, first, 0), (16, 2, 256)) for v in (a_s, b_s))
    mine = jnp.concatenate([mine_a, mine_b])
    places = table[len(cols) : len(cols) + 32]
    unsort = (lax.iota(jnp.int32, 32)[:, None] == places[None, :]).astype(bf16)
    mine = jnp.dot(unsort, mine.reshape(32, 512), preferred_element_type=f32)
    mine = mine.reshape(32, 2, 256).transpose(1, 0, 2).reshape(2, 8192)
    error = jnp.mean((full - mine) ** 2, axis=1)
    return stream_out, codes_out, full.astype(bf16), error


def solution(mesh):
    fine = Mesh(mesh.devices.reshape(SIZES), AXES)
    return jax.shard_map(
        step,
        mesh=fine,
        in_specs=(
            P(LAT, TP),
            P(TP, None),
            P(LAT + TP, None),
            P(),
            P(None, TP + LAT),
            P(TP + LAT),
            P(TP + LAT),
            P(),
        ),
        out_specs=(
            P(LAT + TP, None),
            P(None, TP + LAT),
            P(TP + LAT, None),
            P(TP + LAT),
        ),
        check_vma=False,
    )
```

profile of v0, /device:TPU:24, one launch (start us, length us, event | category | flops | bytes accessed | tf_op | source)
XLA Modules:
  0.0 163.5 jit_solution(9881119351967073624)
XLA Ops:
  1.0 5.9 %project.1 = (bf16[4,128,512]{2,1,0:T(8,128)(2,1)S(1)}, bf16[2,128,512]{2,1,0:T(8,128)(2,1)S(1)}, bf16[2,128,512]{2,1,0:T(8,128)(2,1)S(1)}, bf16[2,128,512]{2,1,...) custom-call(s32[87]{0:T(128)S(1)} %stack.402.cols_ref.table_ref, bf16[128,512]{1,0:T(8,128)(2,1)} %attn_hbm.1, ...), custom_call_target="tpu_custom_call" | custom-call | tf_op jit(solution)/shard_map/project/pallas_call | solution.py:119
  6.9 1.6 collective-permute-start
  8.4 0.7 collective-permute-start.6
  9.2 2.5 %collective-permute-start.5 = (bf16[2,128,512]{2,1,0:T(8,128)(2,1)S(1)}, bf16[2,128,512]{2,1,0:T(8,128)(2,1)}, u32[]{:S(2)}, u32[]{:S(2)}) collective-permute-start(bf16[2,128,512]{2,1,0:T(8,128)(2,1)S(1)} %get-tuple-element.23), channel_id=1, source_target_pairs={{0,32},{32,64},{64,96},{96,0},{1,33},{33,65},{65,97},{97,1},{2,34}... | collective-permute-start | bytes 786440 | tf_op jit(solution)/shard_map/ppermute | solution.py:26
  12.9 10.2 %collective-permute-done.6 = bf16[2,128,512]{2,1,0:T(8,128)(2,1)} collective-permute-done((bf16[2,128,512]{2,1,0:T(8,128)(2,1)S(1)}, bf16[2,128,512]{2,1,0:T(8,128)(2,1)}, u32[]{:S(2)}, u32[]{:S(2)}) %collective-permute-start.6) | collective-permute-done | bytes 262176 | tf_op jit(solution)/shard_map/ppermute | solution.py:26
  23.2 1.1 fusion.15
  24.3 0.6 collective-permute-start.7
  25.0 0.9 collective-permute-start.3
  25.9 2.4 %collective-permute-start.2 = (bf16[128,512]{1,0:T(8,128)(2,1)S(1)}, bf16[128,512]{1,0:T(8,128)(2,1)S(1)}, u32[]{:S(2)}, u32[]{:S(2)}) collective-permute-start(bf16[128,512]{1,0:T(8,128)(2,1)S(1)} %get-tuple-element.38), channel_id=1, source_target_pairs={{0,32},{32,64},{64,96},{96,0},{1,33},{33,65},{65,97},{97,1},{2,34}... | collective-permute-start | bytes 393224 | tf_op jit(solution)/shard_map/ppermute | solution.py:26
  28.3 1.2 collective-permute-start.1
  29.5 1.1 fusion.7
  30.7 1.9 %collective-permute-done.3 = bf16[128,512]{1,0:T(8,128)(2,1)S(1)} collective-permute-done((bf16[128,512]{1,0:T(8,128)(2,1)S(1)}, bf16[128,512]{1,0:T(8,128)(2,1)S(1)}, u32[]{:S(2)}, u32[]{:S(2)}) %collective-permute-start.3) | collective-permute-done | bytes 131104 | tf_op jit(solution)/shard_map/ppermute | solution.py:26
  32.7 2.1 %collective-permute-done.1 = bf16[128,512]{1,0:T(8,128)(2,1)S(1)} collective-permute-done((bf16[128,512]{1,0:T(8,128)(2,1)S(1)}, bf16[128,512]{1,0:T(8,128)(2,1)S(1)}, u32[]{:S(2)}, u32[]{:S(2)}) %collective-permute-start.1) | collective-permute-done | bytes 131104 | tf_op jit(solution)/shard_map/ppermute | solution.py:26
  35.8 3.1 %collective-permute-start.9 = (bf16[128,512]{1,0:T(8,128)(2,1)S(1)}, bf16[128,512]{1,0:T(8,128)(2,1)S(1)}, u32[]{:S(2)}, u32[]{:S(2)}) collective-permute-start(bf16[128,512]{1,0:T(8,128)(2,1)S(1)} %convolution_convert_fusion.1), channel_id=1, source_target_pairs={{0,8},{8,0},{1,9},{9,1},{2,10},{10,2},{3,11},{11,3},{4,12},{12,4},... | collective-permute-start | bytes 393224 | tf_op jit(solution)/shard_map/ppermute | solution.py:26
  38.9 0.3 collective-permute-start.8
  39.3 4.0 %collective-permute-done.9 = bf16[128,512]{1,0:T(8,128)(2,1)S(1)} collective-permute-done((bf16[128,512]{1,0:T(8,128)(2,1)S(1)}, bf16[128,512]{1,0:T(8,128)(2,1)S(1)}, u32[]{:S(2)}, u32[]{:S(2)}) %collective-permute-start.9) | collective-permute-done | bytes 131104 | tf_op jit(solution)/shard_map/ppermute | solution.py:26
  43.3 2.5 %collective-permute-done.8 = bf16[128,512]{1,0:T(8,128)(2,1)S(1)} collective-permute-done((bf16[128,512]{1,0:T(8,128)(2,1)S(1)}, bf16[128,512]{1,0:T(8,128)(2,1)S(1)}, u32[]{:S(2)}, u32[]{:S(2)}) %collective-permute-start.8) | collective-permute-done | bytes 131104 | tf_op jit(solution)/shard_map/ppermute | solution.py:246
  46.1 4.1 %collective-permute-start.13 = (bf16[128,512]{1,0:T(8,128)(2,1)S(1)}, bf16[128,512]{1,0:T(8,128)(2,1)S(1)}, u32[]{:S(2)}, u32[]{:S(2)}) collective-permute-start(bf16[128,512]{1,0:T(8,128)(2,1)S(1)} %fusion.2), channel_id=1, source_target_pairs={{0,6},{2,0},{4,2},{6,4},{1,7},{3,1},{5,3},{7,5},{8,14},{10,8},{12,... | collective-permute-start | bytes 393224 | tf_op jit(solution)/shard_map/ppermute | solution.py:26
  50.2 1.9 %collective-permute-start.11 = (bf16[128,512]{1,0:T(8,128)(2,1)S(1)}, bf16[128,512]{1,0:T(8,128)(2,1)S(1)}, u32[]{:S(2)}, u32[]{:S(2)}) collective-permute-start(bf16[128,512]{1,0:T(8,128)(2,1)S(1)} %fusion.2), channel_id=1, source_target_pairs={{0,4},{2,6},{4,0},{6,2},{1,5},{3,7},{5,1},{7,3},{8,12},{10,14},{12... | collective-permute-start | bytes 393224 | tf_op jit(solution)/shard_map/ppermute | solution.py:26
  52.1 1.4 collective-permute-start.14
  53.4 6.1 %collective-permute-done.12 = bf16[128,512]{1,0:T(8,128)(2,1)S(1)} collective-permute-done((bf16[128,512]{1,0:T(8,128)(2,1)S(1)}, bf16[128,512]{1,0:T(8,128)(2,1)S(1)}, u32[]{:S(2)}, u32[]{:S(2)}) %collective-permute-start.12) | collective-permute-done | bytes 131104 | tf_op jit(solution)/shard_map/ppermute | solution.py:26
  59.9 1.4 collective-permute-start.18
  61.4 0.6 collective-permute-start.24
  62.0 2.3 %collective-permute-done.18 = bf16[128,256]{1,0:T(8,128)(2,1)S(1)} collective-permute-done((bf16[128,256]{1,0:T(8,128)(2,1)S(1)}, bf16[128,256]{1,0:T(8,128)(2,1)S(1)}, u32[]{:S(2)}, u32[]{:S(2)}) %collective-permute-start.18) | collective-permute-done | bytes 65568 | tf_op jit(solution)/shard_map/ppermute | solution.py:61
  64.2 3.0 %collective-permute-start.19 = (bf16[2,128,256]{2,1,0:T(8,128)(2,1)S(1)}, bf16[2,128,256]{2,1,0:T(8,128)(2,1)S(1)}, u32[]{:S(2)}, u32[]{:S(2)}) collective-permute-start(bf16[2,128,256]{2,1,0:T(8,128)(2,1)S(1)} %pad_maximum_fusion.5), channel_id=1, source_target_pairs={{0,8},{16,24},{8,0},{24,16},{1,9},{17,25},{9,1},{25,17},{2,10},{18... | collective-permute-start | bytes 393224 | tf_op jit(solution)/shard_map/ppermute | solution.py:61
  67.2 1.3 collective-permute-start.25
  68.5 2.3 %collective-permute-done.19 = bf16[2,128,256]{2,1,0:T(8,128)(2,1)S(1)} collective-permute-done((bf16[2,128,256]{2,1,0:T(8,128)(2,1)S(1)}, bf16[2,128,256]{2,1,0:T(8,128)(2,1)S(1)}, u32[]{:S(2)}, u32[]{:S(2)}) %collective-permute-start.19) | collective-permute-done | bytes 131104 | tf_op jit(solution)/shard_map/ppermute | solution.py:61
  70.8 0.5 collective-permute-start.22
  71.4 0.7 collective-permute-start.17
  72.1 3.6 %collective-permute-start.16 = (bf16[2,16,1024]{2,1,0:T(8,128)(2,1)S(1)}, bf16[2,16,1024]{2,1,0:T(8,128)(2,1)S(1)}, u32[]{:S(2)}, u32[]{:S(2)}) collective-permute-start(bf16[2,16,1024]{2,1,0:T(8,128)(2,1)S(1)} %get-tuple-element.53), channel_id=1, source_target_pairs={{0,64},{32,96},{64,0},{96,32},{1,65},{33,97},{65,1},{97,33},{2,66}... | collective-permute-start | bytes 196616 | tf_op jit(solution)/shard_map/ppermute | solution.py:26
  75.7 1.1 collective-permute-start.15
  76.8 0.8 collective-permute-start.21
  77.7 5.0 %collective-permute-done.17 = bf16[2,16,1024]{2,1,0:T(8,128)(2,1)S(1)} collective-permute-done((bf16[2,16,1024]{2,1,0:T(8,128)(2,1)S(1)}, bf16[2,16,1024]{2,1,0:T(8,128)(2,1)S(1)}, u32[]{:S(2)}, u32[]{:S(2)}) %collective-permute-start.17) | collective-permute-done | bytes 65568 | tf_op jit(solution)/shard_map/ppermute | solution.py:26
  82.7 0.5 collective-permute-start.20
  83.2 0.9 collective-permute-done.16
  84.1 2.1 %collective-permute-start.28 = (bf16[4,128,256]{2,1,0:T(8,128)(2,1)S(1)}, bf16[4,128,256]{2,1,0:T(8,128)(2,1)S(1)}, u32[]{:S(2)}, u32[]{:S(2)}) collective-permute-start(bf16[4,128,256]{2,1,0:T(8,128)(2,1)S(1)} %get-tuple-element.46), channel_id=1, source_target_pairs={{0,24},{16,0},{8,16},{24,8},{1,25},{17,1},{9,17},{25,9},{2,26},{18... | collective-permute-start | bytes 786440 | tf_op jit(solution)/shard_map/ppermute | solution.py:24
  86.2 1.3 collective-permute-start.27
  87.9 1.2 collective-permute-done.20
  89.3 3.6 %collective-permute-done.28 = bf16[4,128,256]{2,1,0:T(8,128)(2,1)S(1)} collective-permute-done((bf16[4,128,256]{2,1,0:T(8,128)(2,1)S(1)}, bf16[4,128,256]{2,1,0:T(8,128)(2,1)S(1)}, u32[]{:S(2)}, u32[]{:S(2)}) %collective-permute-start.28) | collective-permute-done | bytes 262176 | tf_op jit(solution)/shard_map/ppermute | solution.py:24
  92.9 1.2 collective-permute-done.27
  94.1 2.7 %collective-permute-done.26 = bf16[4,128,256]{2,1,0:T(8,128)(2,1)S(1)} collective-permute-done((bf16[4,128,256]{2,1,0:T(8,128)(2,1)S(1)}, bf16[4,128,256]{2,1,0:T(8,128)(2,1)S(1)}, u32[]{:S(2)}, u32[]{:S(2)}) %collective-permute-start.26) | collective-permute-done | bytes 262176 | tf_op jit(solution)/shard_map/ppermute | solution.py:24
  97.3 2.4 %collective-permute-done.29.tb_ref = bf16[4,4,128,256]{3,2,1,0:T(8,128)(2,1)S(1)} collective-permute-done((bf16[4,4,128,256]{3,2,1,0:T(8,128)(2,1)S(1)}, bf16[4,4,128,256]{3,2,1,0:T(8,128)(2,1)S(1)}, u32[]{:S(2)}, u32[]{:S(2)}) %collective-permute-start.29) | collective-permute-done | bytes 1048608 | tf_op jit(solution)/shard_map/ppermute | solution.py:26
  99.7 13.5 %autoencode.1 = (bf16[256,1024]{1,0:T(8,128)(2,1)}, f32[128,4096]{1,0:T(8,128)S(1)}, bf16[128,4096]{1,0:T(8,128)(2,1)S(1)}, f32[128,4096]{1,0:T(8,128)S(1)}, bf16[128,4096]{1,0:T(8,128)(2,1)S(1)}) custom-call(s32[87]{0:T(128)S(1)} %stack.402.cols_ref.table_ref, bf16[4,4,128,256]{3,2,1,0:T(8,128)(2,1)S(1)} %pad_maximum_fusion.oa_ref, ...), custom_call_target="tpu_custom_call" | custom-call | tf_op jit(solution)/shard_map/autoencode/pallas_call | solution.py:175
  113.6 0.5 collective-permute-start.36
  114.2 1.9 %collective-permute-done.30 = bf16[128,4096]{1,0:T(8,128)(2,1)S(1)} collective-permute-done((bf16[128,4096]{1,0:T(8,128)(2,1)S(1)}, bf16[128,4096]{1,0:T(8,128)(2,1)S(1)}, u32[]{:S(2)}, u32[]{:S(2)}) %collective-permute-start.30) | collective-permute-done | bytes 1048608 | tf_op jit(solution)/shard_map/ppermute | solution.py:26
  116.0 0.2 add_convert_fusion.1
  116.3 1.5 collective-permute-start.33
  117.8 2.1 %collective-permute-start.32 = (bf16[4,8,4096]{2,1,0:T(8,128)(2,1)S(1)}, bf16[4,8,4096]{2,1,0:T(8,128)(2,1)S(1)}, u32[]{:S(2)}, u32[]{:S(2)}) collective-permute-start(bf16[4,8,4096]{2,1,0:T(8,128)(2,1)S(1)} %get-tuple-element.44), channel_id=1, source_target_pairs={{0,32},{32,64},{64,96},{96,0},{1,33},{33,65},{65,97},{97,1},{2,34}... | collective-permute-start | bytes 786440 | tf_op jit(solution)/shard_map/ppermute | solution.py:26
  120.0 0.2 add_convert_fusion
  120.3 0.7 collective-permute-start.39
  121.0 1.4 collective-permute-start.38
  122.4 9.4 %collective-permute-done.33 = bf16[4,8,4096]{2,1,0:T(8,128)(2,1)S(1)} collective-permute-done((bf16[4,8,4096]{2,1,0:T(8,128)(2,1)S(1)}, bf16[4,8,4096]{2,1,0:T(8,128)(2,1)S(1)}, u32[]{:S(2)}, u32[]{:S(2)}) %collective-permute-start.33) | collective-permute-done | bytes 262176 | tf_op jit(solution)/shard_map/ppermute | solution.py:26
  131.8 1.3 collective-permute-start.37
  133.5 8.7 %collective-permute-done.37 = bf16[4,8,4096]{2,1,0:T(8,128)(2,1)S(1)} collective-permute-done((bf16[4,8,4096]{2,1,0:T(8,128)(2,1)S(1)}, bf16[4,8,4096]{2,1,0:T(8,128)(2,1)S(1)}, u32[]{:S(2)}, u32[]{:S(2)}) %collective-permute-start.37) | collective-permute-done | bytes 262176 | tf_op jit(solution)/shard_map/ppermute | solution.py:24
  142.5 1.7 %collective-permute-start.35 = (bf16[8,4096]{1,0:T(8,128)(2,1)S(1)}, bf16[8,4096]{1,0:T(8,128)(2,1)S(1)}, u32[]{:S(2)}, u32[]{:S(2)}) collective-permute-start(bf16[8,4096]{1,0:T(8,128)(2,1)S(1)} %fusion.30), channel_id=1, source_target_pairs={{0,8},{16,24},{8,0},{24,16},{1,9},{17,25},{9,1},{25,17},{2,10},{18... | collective-permute-start | bytes 196616 | tf_op jit(solution)/shard_map/ppermute | solution.py:61
  144.2 3.2 %collective-permute-done.40 = bf16[2,8,4096]{2,1,0:T(8,128)(2,1)S(1)} collective-permute-done((bf16[2,8,4096]{2,1,0:T(8,128)(2,1)S(1)}, bf16[2,8,4096]{2,1,0:T(8,128)(2,1)S(1)}, u32[]{:S(2)}, u32[]{:S(2)}) %collective-permute-start.40) | collective-permute-done | bytes 131104 | tf_op jit(solution)/shard_map/ppermute | solution.py:62
  147.6 0.8 collective-permute-done.35
  148.5 4.8 %collective-permute-done.41 = bf16[8,4096]{1,0:T(8,128)(2,1)S(1)} collective-permute-done((bf16[8,4096]{1,0:T(8,128)(2,1)S(1)}, bf16[8,4096]{1,0:T(8,128)(2,1)S(1)}, u32[]{:S(2)}, u32[]{:S(2)}) %collective-permute-start.41) | collective-permute-done | bytes 65568 | tf_op jit(solution)/shard_map/ppermute | solution.py:62
  153.5 3.1 %collective-permute-start.44 = (bf16[2,8192]{1,0:T(2,128)(2,1)S(1)}, bf16[2,8192]{1,0:T(2,128)(2,1)S(1)}, u32[]{:S(2)}, u32[]{:S(2)}) collective-permute-start(bf16[2,8192]{1,0:T(2,128)(2,1)S(1)} %get-tuple-element.60), channel_id=1, source_target_pairs={{0,6},{2,0},{4,2},{6,4},{1,7},{3,1},{5,3},{7,5},{8,14},{10,8},{12,... | collective-permute-start | bytes 98312 | tf_op jit(solution)/shard_map/ppermute | solution.py:26
  156.7 1.5 collective-permute-start.42
  158.4 3.4 %collective-permute-done.43 = bf16[2,8192]{1,0:T(2,128)(2,1)S(1)} collective-permute-done((bf16[2,8192]{1,0:T(2,128)(2,1)S(1)}, bf16[2,8192]{1,0:T(2,128)(2,1)S(1)}, u32[]{:S(2)}, u32[]{:S(2)}) %collective-permute-start.43) | collective-permute-done | bytes 32800 | tf_op jit(solution)/shard_map/ppermute | solution.py:26
  161.8 0.3 collective-permute-done.42
  162.1 0.8 multiply_reduce_fusion
  163.0 0.5 broadcast_multiply_fusion
  (126 shorter events, 6.2 us)
Async XLA Ops:
  1.0 11.6 %copy-start.3 = (s32[256]{0:T(256)S(1)}, s32[256]{0:T(256)}, u32[]{:S(2)}) copy-start(s32[256]{0:T(256)} %param.11) | copy-start | bytes 3076
  6.9 18.0 %collective-permute-start = (bf16[4,128,512]{2,1,0:T(8,128)(2,1)S(1)}, bf16[4,128,512]{2,1,0:T(8,128)(2,1)S(1)}, u32[]{:S(2)}, u32[]{:S(2)}) collective-permute-start(bf16[4,128,512]{2,1,0:T(8,128)(2,1)S(1)} %get-tuple-element.20), channel_id=1, source_target_pairs={{0,16},{16,0},{1,17},{17,1},{2,18},{18,2},{3,19},{19,3},{4,20},{20... | collective-permute-start | bytes 1572872 | tf_op jit(solution)/shard_map/ppermute | solution.py:26
  8.4 14.7 %collective-permute-start.6 = (bf16[2,128,512]{2,1,0:T(8,128)(2,1)S(1)}, bf16[2,128,512]{2,1,0:T(8,128)(2,1)}, u32[]{:S(2)}, u32[]{:S(2)}) collective-permute-start(bf16[2,128,512]{2,1,0:T(8,128)(2,1)S(1)} %get-tuple-element.24), channel_id=1, source_target_pairs={{0,96},{32,0},{64,32},{96,64},{1,97},{33,1},{65,33},{97,65},{2,98}... | collective-permute-start | bytes 786440 | tf_op jit(solution)/shard_map/ppermute | solution.py:26
  9.2 14.0 %collective-permute-start.5 = (bf16[2,128,512]{2,1,0:T(8,128)(2,1)S(1)}, bf16[2,128,512]{2,1,0:T(8,128)(2,1)}, u32[]{:S(2)}, u32[]{:S(2)}) collective-permute-start(bf16[2,128,512]{2,1,0:T(8,128)(2,1)S(1)} %get-tuple-element.23), channel_id=1, source_target_pairs={{0,32},{32,64},{64,96},{96,0},{1,33},{33,65},{65,97},{97,1},{2,34}... | collective-permute-start | bytes 786440 | tf_op jit(solution)/shard_map/ppermute | solution.py:26
  11.7 11.5 %collective-permute-start.4 = (bf16[2,128,512]{2,1,0:T(8,128)(2,1)S(1)}, bf16[2,128,512]{2,1,0:T(8,128)(2,1)}, u32[]{:S(2)}, u32[]{:S(2)}) collective-permute-start(bf16[2,128,512]{2,1,0:T(8,128)(2,1)S(1)} %get-tuple-element.22), channel_id=1, source_target_pairs={{0,64},{32,96},{64,0},{96,32},{1,65},{33,97},{65,1},{97,33},{2,66}... | collective-permute-start | bytes 786440 | tf_op jit(solution)/shard_map/ppermute | solution.py:26
  24.3 5.2 %collective-permute-start.7 = (bf16[128,512]{1,0:T(8,128)(2,1)S(1)}, bf16[128,512]{1,0:T(8,128)(2,1)S(1)}, u32[]{:S(2)}, u32[]{:S(2)}) collective-permute-start(bf16[128,512]{1,0:T(8,128)(2,1)S(1)} %fusion.15), channel_id=1, source_target_pairs={{0,16},{16,0},{1,17},{17,1},{2,18},{18,2},{3,19},{19,3},{4,20},{20... | collective-permute-start | bytes 393224 | tf_op jit(solution)/shard_map/ppermute | solution.py:26
  25.0 7.7 %collective-permute-start.3 = (bf16[128,512]{1,0:T(8,128)(2,1)S(1)}, bf16[128,512]{1,0:T(8,128)(2,1)S(1)}, u32[]{:S(2)}, u32[]{:S(2)}) collective-permute-start(bf16[128,512]{1,0:T(8,128)(2,1)S(1)} %get-tuple-element.37), channel_id=1, source_target_pairs={{0,96},{32,0},{64,32},{96,64},{1,97},{33,1},{65,33},{97,65},{2,98}... | collective-permute-start | bytes 393224 | tf_op jit(solution)/shard_map/ppermute | solution.py:26
  25.9 6.7 %collective-permute-start.2 = (bf16[128,512]{1,0:T(8,128)(2,1)S(1)}, bf16[128,512]{1,0:T(8,128)(2,1)S(1)}, u32[]{:S(2)}, u32[]{:S(2)}) collective-permute-start(bf16[128,512]{1,0:T(8,128)(2,1)S(1)} %get-tuple-element.38), channel_id=1, source_target_pairs={{0,32},{32,64},{64,96},{96,0},{1,33},{33,65},{65,97},{97,1},{2,34}... | collective-permute-start | bytes 393224 | tf_op jit(solution)/shard_map/ppermute | solution.py:26
  28.3 6.5 %collective-permute-start.1 = (bf16[128,512]{1,0:T(8,128)(2,1)S(1)}, bf16[128,512]{1,0:T(8,128)(2,1)S(1)}, u32[]{:S(2)}, u32[]{:S(2)}) collective-permute-start(bf16[128,512]{1,0:T(8,128)(2,1)S(1)} %get-tuple-element.36), channel_id=1, source_target_pairs={{0,64},{32,96},{64,0},{96,32},{1,65},{33,97},{65,1},{97,33},{2,66}... | collective-permute-start | bytes 393224 | tf_op jit(solution)/shard_map/ppermute | solution.py:26
  35.3 4.0 %collective-permute-start.10 = (bf16[128,512]{1,0:T(8,128)(2,1)S(1)}, bf16[128,512]{1,0:T(8,128)(2,1)S(1)}, u32[]{:S(2)}, u32[]{:S(2)}) collective-permute-start(bf16[128,512]{1,0:T(8,128)(2,1)S(1)} %convolution_convert_fusion), channel_id=1, source_target_pairs={{0,1},{1,0},{2,3},{3,2},{4,5},{5,4},{6,7},{7,6},{8,9},{9,8},{10,11... | collective-permute-start | bytes 393224 | tf_op jit(solution)/shard_map/ppermute | solution.py:26
  35.8 7.5 %collective-permute-start.9 = (bf16[128,512]{1,0:T(8,128)(2,1)S(1)}, bf16[128,512]{1,0:T(8,128)(2,1)S(1)}, u32[]{:S(2)}, u32[]{:S(2)}) collective-permute-start(bf16[128,512]{1,0:T(8,128)(2,1)S(1)} %convolution_convert_fusion.1), channel_id=1, source_target_pairs={{0,8},{8,0},{1,9},{9,1},{2,10},{10,2},{3,11},{11,3},{4,12},{12,4},... | collective-permute-start | bytes 393224 | tf_op jit(solution)/shard_map/ppermute | solution.py:26
  38.9 6.9 %collective-permute-start.8 = (bf16[128,512]{1,0:T(8,128)(2,1)S(1)}, bf16[128,512]{1,0:T(8,128)(2,1)S(1)}, u32[]{:S(2)}, u32[]{:S(2)}) collective-permute-start(bf16[128,512]{1,0:T(8,128)(2,1)S(1)} %convolution_convert_fusion.2), channel_id=1, source_target_pairs={{0,9},{1,8},{8,1},{9,0},{2,11},{3,10},{10,3},{11,2},{4,13},{5,12},... | collective-permute-start | bytes 393224 | tf_op jit(solution)/shard_map/ppermute | solution.py:246
  46.1 7.4 %collective-permute-start.13 = (bf16[128,512]{1,0:T(8,128)(2,1)S(1)}, bf16[128,512]{1,0:T(8,128)(2,1)S(1)}, u32[]{:S(2)}, u32[]{:S(2)}) collective-permute-start(bf16[128,512]{1,0:T(8,128)(2,1)S(1)} %fusion.2), channel_id=1, source_target_pairs={{0,6},{2,0},{4,2},{6,4},{1,7},{3,1},{5,3},{7,5},{8,14},{10,8},{12,... | collective-permute-start | bytes 393224 | tf_op jit(solution)/shard_map/ppermute | solution.py:26
  50.2 9.4 %collective-permute-start.12 = (bf16[128,512]{1,0:T(8,128)(2,1)S(1)}, bf16[128,512]{1,0:T(8,128)(2,1)S(1)}, u32[]{:S(2)}, u32[]{:S(2)}) collective-permute-start(bf16[128,512]{1,0:T(8,128)(2,1)S(1)} %fusion.2), channel_id=1, source_target_pairs={{0,2},{2,4},{4,6},{6,0},{1,3},{3,5},{5,7},{7,1},{8,10},{10,12},{12... | collective-permute-start | bytes 393224 | tf_op jit(solution)/shard_map/ppermute | solution.py:26
  50.2 9.4 %collective-permute-start.11 = (bf16[128,512]{1,0:T(8,128)(2,1)S(1)}, bf16[128,512]{1,0:T(8,128)(2,1)S(1)}, u32[]{:S(2)}, u32[]{:S(2)}) collective-permute-start(bf16[128,512]{1,0:T(8,128)(2,1)S(1)} %fusion.2), channel_id=1, source_target_pairs={{0,4},{2,6},{4,0},{6,2},{1,5},{3,7},{5,1},{7,3},{8,12},{10,14},{12... | collective-permute-start | bytes 393224 | tf_op jit(solution)/shard_map/ppermute | solution.py:26
  52.1 7.5 %collective-permute-start.14 = (bf16[4,16,1024]{2,1,0:T(8,128)(2,1)S(1)}, bf16[4,16,1024]{2,1,0:T(8,128)(2,1)S(1)}, u32[]{:S(2)}, u32[]{:S(2)}) collective-permute-start(bf16[4,16,1024]{2,1,0:T(8,128)(2,1)S(1)} %get-tuple-element.55), channel_id=1, source_target_pairs={{0,16},{16,0},{1,17},{17,1},{2,18},{18,2},{3,19},{19,3},{4,20},{20... | collective-permute-start | bytes 393224 | tf_op jit(solution)/shard_map/ppermute | solution.py:26
  59.9 4.3 %collective-permute-start.18 = (bf16[128,256]{1,0:T(8,128)(2,1)S(1)}, bf16[128,256]{1,0:T(8,128)(2,1)S(1)}, u32[]{:S(2)}, u32[]{:S(2)}) collective-permute-start(bf16[128,256]{1,0:T(8,128)(2,1)S(1)} %bitcast.295), channel_id=1, source_target_pairs={{0,16},{16,0},{8,24},{24,8},{1,17},{17,1},{9,25},{25,9},{2,18},{18... | collective-permute-start | bytes 196616 | tf_op jit(solution)/shard_map/ppermute | solution.py:61
  61.4 5.8 %collective-permute-start.24 = (bf16[128,256]{1,0:T(8,128)(2,1)S(1)}, bf16[128,256]{1,0:T(8,128)(2,1)S(1)}, u32[]{:S(2)}, u32[]{:S(2)}) collective-permute-start(bf16[128,256]{1,0:T(8,128)(2,1)S(1)} %bitcast.292), channel_id=1, source_target_pairs={{0,32},{32,0},{64,96},{96,64},{1,33},{33,1},{65,97},{97,65},{2,34}... | collective-permute-start | bytes 196616 | tf_op jit(solution)/shard_map/ppermute | solution.py:62
  64.2 6.6 %collective-permute-start.19 = (bf16[2,128,256]{2,1,0:T(8,128)(2,1)S(1)}, bf16[2,128,256]{2,1,0:T(8,128)(2,1)S(1)}, u32[]{:S(2)}, u32[]{:S(2)}) collective-permute-start(bf16[2,128,256]{2,1,0:T(8,128)(2,1)S(1)} %pad_maximum_fusion.5), channel_id=1, source_target_pairs={{0,8},{16,24},{8,0},{24,16},{1,9},{17,25},{9,1},{25,17},{2,10},{18... | collective-permute-start | bytes 393224 | tf_op jit(solution)/shard_map/ppermute | solution.py:61
  67.2 9.6 %collective-permute-start.25 = (bf16[2,128,256]{2,1,0:T(8,128)(2,1)S(1)}, bf16[2,128,256]{2,1,0:T(8,128)(2,1)S(1)}, u32[]{:S(2)}, u32[]{:S(2)}) collective-permute-start(bf16[2,128,256]{2,1,0:T(8,128)(2,1)S(1)} %pad_maximum_fusion.6), channel_id=1, source_target_pairs={{0,64},{32,96},{64,0},{96,32},{1,65},{33,97},{65,1},{97,33},{2,66}... | collective-permute-start | bytes 393224 | tf_op jit(solution)/shard_map/ppermute | solution.py:62
  70.8 16.7 %collective-permute-start.22 = (bf16[4,128,256]{2,1,0:T(8,128)(2,1)S(1)}, bf16[4,128,256]{2,1,0:T(8,128)(2,1)S(1)}, u32[]{:S(2)}, u32[]{:S(2)}) collective-permute-start(bf16[4,128,256]{2,1,0:T(8,128)(2,1)S(1)} %get-tuple-element.48), channel_id=1, source_target_pairs={{0,96},{32,0},{64,32},{96,64},{1,97},{33,1},{65,33},{97,65},{2,98}... | collective-permute-start | bytes 786440 | tf_op jit(solution)/shard_map/ppermute | solution.py:26
  71.4 11.3 %collective-permute-start.17 = (bf16[2,16,1024]{2,1,0:T(8,128)(2,1)S(1)}, bf16[2,16,1024]{2,1,0:T(8,128)(2,1)S(1)}, u32[]{:S(2)}, u32[]{:S(2)}) collective-permute-start(bf16[2,16,1024]{2,1,0:T(8,128)(2,1)S(1)} %get-tuple-element.54), channel_id=1, source_target_pairs={{0,96},{32,0},{64,32},{96,64},{1,97},{33,1},{65,33},{97,65},{2,98}... | collective-permute-start | bytes 196616 | tf_op jit(solution)/shard_map/ppermute | solution.py:26
  72.1 12.0 %collective-permute-start.16 = (bf16[2,16,1024]{2,1,0:T(8,128)(2,1)S(1)}, bf16[2,16,1024]{2,1,0:T(8,128)(2,1)S(1)}, u32[]{:S(2)}, u32[]{:S(2)}) collective-permute-start(bf16[2,16,1024]{2,1,0:T(8,128)(2,1)S(1)} %get-tuple-element.53), channel_id=1, source_target_pairs={{0,64},{32,96},{64,0},{96,32},{1,65},{33,97},{65,1},{97,33},{2,66}... | collective-permute-start | bytes 196616 | tf_op jit(solution)/shard_map/ppermute | solution.py:26
  75.7 10.5 %collective-permute-start.15 = (bf16[2,16,1024]{2,1,0:T(8,128)(2,1)S(1)}, bf16[2,16,1024]{2,1,0:T(8,128)(2,1)S(1)}, u32[]{:S(2)}, u32[]{:S(2)}) collective-permute-start(bf16[2,16,1024]{2,1,0:T(8,128)(2,1)S(1)} %get-tuple-element.52), channel_id=1, source_target_pairs={{0,32},{32,64},{64,96},{96,0},{1,33},{33,65},{65,97},{97,1},{2,34}... | collective-permute-start | bytes 196616 | tf_op jit(solution)/shard_map/ppermute | solution.py:26
  76.8 11.0 %collective-permute-start.21 = (bf16[4,128,256]{2,1,0:T(8,128)(2,1)S(1)}, bf16[4,128,256]{2,1,0:T(8,128)(2,1)S(1)}, u32[]{:S(2)}, u32[]{:S(2)}) collective-permute-start(bf16[4,128,256]{2,1,0:T(8,128)(2,1)S(1)} %get-tuple-element.48), channel_id=1, source_target_pairs={{0,64},{32,96},{64,0},{96,32},{1,65},{33,97},{65,1},{97,33},{2,66}... | collective-permute-start | bytes 786440 | tf_op jit(solution)/shard_map/ppermute | solution.py:26
  82.7 6.4 %collective-permute-start.20 = (bf16[4,128,256]{2,1,0:T(8,128)(2,1)S(1)}, bf16[4,128,256]{2,1,0:T(8,128)(2,1)S(1)}, u32[]{:S(2)}, u32[]{:S(2)}) collective-permute-start(bf16[4,128,256]{2,1,0:T(8,128)(2,1)S(1)} %get-tuple-element.48), channel_id=1, source_target_pairs={{0,32},{32,64},{64,96},{96,0},{1,33},{33,65},{65,97},{97,1},{2,34}... | collective-permute-start | bytes 786440 | tf_op jit(solution)/shard_map/ppermute | solution.py:26
  84.1 8.8 %collective-permute-start.28 = (bf16[4,128,256]{2,1,0:T(8,128)(2,1)S(1)}, bf16[4,128,256]{2,1,0:T(8,128)(2,1)S(1)}, u32[]{:S(2)}, u32[]{:S(2)}) collective-permute-start(bf16[4,128,256]{2,1,0:T(8,128)(2,1)S(1)} %get-tuple-element.46), channel_id=1, source_target_pairs={{0,24},{16,0},{8,16},{24,8},{1,25},{17,1},{9,17},{25,9},{2,26},{18... | collective-permute-start | bytes 786440 | tf_op jit(solution)/shard_map/ppermute | solution.py:24
  86.2 8.0 %collective-permute-start.27 = (bf16[4,128,256]{2,1,0:T(8,128)(2,1)S(1)}, bf16[4,128,256]{2,1,0:T(8,128)(2,1)S(1)}, u32[]{:S(2)}, u32[]{:S(2)}) collective-permute-start(bf16[4,128,256]{2,1,0:T(8,128)(2,1)S(1)} %get-tuple-element.46), channel_id=1, source_target_pairs={{0,8},{16,24},{8,0},{24,16},{1,9},{17,25},{9,1},{25,17},{2,10},{18... | collective-permute-start | bytes 786440 | tf_op jit(solution)/shard_map/ppermute | solution.py:24
  87.5 9.3 %collective-permute-start.26 = (bf16[4,128,256]{2,1,0:T(8,128)(2,1)S(1)}, bf16[4,128,256]{2,1,0:T(8,128)(2,1)S(1)}, u32[]{:S(2)}, u32[]{:S(2)}) collective-permute-start(bf16[4,128,256]{2,1,0:T(8,128)(2,1)S(1)} %get-tuple-element.46), channel_id=1, source_target_pairs={{0,16},{16,8},{8,24},{24,0},{1,17},{17,9},{9,25},{25,1},{2,18},{18... | collective-permute-start | bytes 786440 | tf_op jit(solution)/shard_map/ppermute | solution.py:24
  89.1 10.7 %copy-start = (f32[8192]{0:T(1024)S(1)}, f32[8192]{0:T(1024)}, u32[]{:S(2)}) copy-start(f32[8192]{0:T(1024)} %param.15) | copy-start | bytes 98308
  89.1 10.7 %copy-start.1 = (f32[1024]{0:T(1024)S(1)}, f32[1024]{0:T(1024)}, u32[]{:S(2)}) copy-start(f32[1024]{0:T(1024)} %param.13) | copy-start | bytes 12292
  89.1 10.7 %copy-start.2 = (f32[1024]{0:T(1024)S(1)}, f32[1024]{0:T(1024)}, u32[]{:S(2)}) copy-start(f32[1024]{0:T(1024)} %param.14) | copy-start | bytes 12292
  89.2 8.1 %collective-permute-start.23 = (bf16[4,4,128,256]{3,2,1,0:T(8,128)(2,1)S(1)}, bf16[4,4,128,256]{3,2,1,0:T(8,128)(2,1)S(1)}, u32[]{:S(2)}, u32[]{:S(2)}) collective-permute-start(bf16[4,4,128,256]{3,2,1,0:T(8,128)(2,1)S(1)} %pad_maximum_fusion.oa_ref), channel_id=1, source_target_pairs={{0,1},{1,0},{2,3},{3,2},{4,5},{5,4},{6,7},{7,6},{8,9},{9,8},{10,11... | collective-permute-start | bytes 3145736 | tf_op jit(solution)/shard_map/ppermute | solution.py:26
  97.0 2.7 %collective-permute-start.29 = (bf16[4,4,128,256]{3,2,1,0:T(8,128)(2,1)S(1)}, bf16[4,4,128,256]{3,2,1,0:T(8,128)(2,1)S(1)}, u32[]{:S(2)}, u32[]{:S(2)}) collective-permute-start(bf16[4,4,128,256]{3,2,1,0:T(8,128)(2,1)S(1)} %pad_maximum_fusion.1.ob_ref), channel_id=1, source_target_pairs={{0,1},{1,0},{2,3},{3,2},{4,5},{5,4},{6,7},{7,6},{8,9},{9,8},{10,11... | collective-permute-start | bytes 3145736 | tf_op jit(solution)/shard_map/ppermute | solution.py:26
  113.3 2.7 %collective-permute-start.30 = (bf16[128,4096]{1,0:T(8,128)(2,1)S(1)}, bf16[128,4096]{1,0:T(8,128)(2,1)S(1)}, u32[]{:S(2)}, u32[]{:S(2)}) collective-permute-start(bf16[128,4096]{1,0:T(8,128)(2,1)S(1)} %get-tuple-element.29), channel_id=1, source_target_pairs={{0,1},{1,0},{2,3},{3,2},{4,5},{5,4},{6,7},{7,6},{8,9},{9,8},{10,11... | collective-permute-start | bytes 3145736 | tf_op jit(solution)/shard_map/ppermute | solution.py:26
  113.6 2.7 %copy-start.4 = (bf16[16,8192]{1,0:T(8,128)(2,1)}, bf16[16,8192]{1,0:T(8,128)(2,1)S(1)}, u32[]{:S(2)}) copy-start(bf16[16,8192]{1,0:T(8,128)(2,1)S(1)} %constant_dynamic-update-slice_fusion) | copy-start | bytes 786436
  113.6 6.4 %collective-permute-start.36 = (bf16[128,4096]{1,0:T(8,128)(2,1)S(1)}, bf16[128,4096]{1,0:T(8,128)(2,1)S(1)}, u32[]{:S(2)}, u32[]{:S(2)}) collective-permute-start(bf16[128,4096]{1,0:T(8,128)(2,1)S(1)} %get-tuple-element.31), channel_id=1, source_target_pairs={{0,1},{1,0},{2,3},{3,2},{4,5},{5,4},{6,7},{7,6},{8,9},{9,8},{10,11... | collective-permute-start | bytes 3145736 | tf_op jit(solution)/shard_map/ppermute | solution.py:26
  116.3 15.5 %collective-permute-start.33 = (bf16[4,8,4096]{2,1,0:T(8,128)(2,1)S(1)}, bf16[4,8,4096]{2,1,0:T(8,128)(2,1)S(1)}, u32[]{:S(2)}, u32[]{:S(2)}) collective-permute-start(bf16[4,8,4096]{2,1,0:T(8,128)(2,1)S(1)} %get-tuple-element.43), channel_id=1, source_target_pairs={{0,96},{32,0},{64,32},{96,64},{1,97},{33,1},{65,33},{97,65},{2,98}... | collective-permute-start | bytes 786440 | tf_op jit(solution)/shard_map/ppermute | solution.py:26
  117.8 15.3 %collective-permute-start.32 = (bf16[4,8,4096]{2,1,0:T(8,128)(2,1)S(1)}, bf16[4,8,4096]{2,1,0:T(8,128)(2,1)S(1)}, u32[]{:S(2)}, u32[]{:S(2)}) collective-permute-start(bf16[4,8,4096]{2,1,0:T(8,128)(2,1)S(1)} %get-tuple-element.44), channel_id=1, source_target_pairs={{0,32},{32,64},{64,96},{96,0},{1,33},{33,65},{65,97},{97,1},{2,34}... | collective-permute-start | bytes 786440 | tf_op jit(solution)/shard_map/ppermute | solution.py:26
  119.9 13.3 %collective-permute-start.31 = (bf16[4,8,4096]{2,1,0:T(8,128)(2,1)S(1)}, bf16[4,8,4096]{2,1,0:T(8,128)(2,1)S(1)}, u32[]{:S(2)}, u32[]{:S(2)}) collective-permute-start(bf16[4,8,4096]{2,1,0:T(8,128)(2,1)S(1)} %get-tuple-element.42), channel_id=1, source_target_pairs={{0,64},{32,96},{64,0},{96,32},{1,65},{33,97},{65,1},{97,33},{2,66}... | collective-permute-start | bytes 786440 | tf_op jit(solution)/shard_map/ppermute | solution.py:26
  120.3 13.2 %collective-permute-start.39 = (bf16[4,8,4096]{2,1,0:T(8,128)(2,1)S(1)}, bf16[4,8,4096]{2,1,0:T(8,128)(2,1)S(1)}, u32[]{:S(2)}, u32[]{:S(2)}) collective-permute-start(bf16[4,8,4096]{2,1,0:T(8,128)(2,1)S(1)} %get-tuple-element.40), channel_id=1, source_target_pairs={{0,24},{16,0},{8,16},{24,8},{1,25},{17,1},{9,17},{25,9},{2,26},{18... | collective-permute-start | bytes 786440 | tf_op jit(solution)/shard_map/ppermute | solution.py:24
  121.0 12.6 %collective-permute-start.38 = (bf16[4,8,4096]{2,1,0:T(8,128)(2,1)S(1)}, bf16[4,8,4096]{2,1,0:T(8,128)(2,1)S(1)}, u32[]{:S(2)}, u32[]{:S(2)}) collective-permute-start(bf16[4,8,4096]{2,1,0:T(8,128)(2,1)S(1)} %get-tuple-element.41), channel_id=1, source_target_pairs={{0,16},{16,8},{8,24},{24,0},{1,17},{17,9},{9,25},{25,1},{2,18},{18... | collective-permute-start | bytes 786440 | tf_op jit(solution)/shard_map/ppermute | solution.py:24
  131.8 10.4 %collective-permute-start.37 = (bf16[4,8,4096]{2,1,0:T(8,128)(2,1)S(1)}, bf16[4,8,4096]{2,1,0:T(8,128)(2,1)S(1)}, u32[]{:S(2)}, u32[]{:S(2)}) collective-permute-start(bf16[4,8,4096]{2,1,0:T(8,128)(2,1)S(1)} %get-tuple-element.39), channel_id=1, source_target_pairs={{0,8},{16,24},{8,0},{24,16},{1,9},{17,25},{9,1},{25,17},{2,10},{18... | collective-permute-start | bytes 786440 | tf_op jit(solution)/shard_map/ppermute | solution.py:24
  133.3 9.2 %collective-permute-start.34 = (bf16[2,8,4096]{2,1,0:T(8,128)(2,1)S(1)}, bf16[2,8,4096]{2,1,0:T(8,128)(2,1)S(1)}, u32[]{:S(2)}, u32[]{:S(2)}) collective-permute-start(bf16[2,8,4096]{2,1,0:T(8,128)(2,1)S(1)} %fusion.16), channel_id=1, source_target_pairs={{0,16},{16,0},{8,24},{24,8},{1,17},{17,1},{9,25},{25,9},{2,18},{18... | collective-permute-start | bytes 393224 | tf_op jit(solution)/shard_map/ppermute | solution.py:61
  142.4 5.0 %collective-permute-start.40 = (bf16[2,8,4096]{2,1,0:T(8,128)(2,1)S(1)}, bf16[2,8,4096]{2,1,0:T(8,128)(2,1)S(1)}, u32[]{:S(2)}, u32[]{:S(2)}) collective-permute-start(bf16[2,8,4096]{2,1,0:T(8,128)(2,1)S(1)} %fusion.17), channel_id=1, source_target_pairs={{0,32},{32,0},{64,96},{96,64},{1,33},{33,1},{65,97},{97,65},{2,34}... | collective-permute-start | bytes 393224 | tf_op jit(solution)/shard_map/ppermute | solution.py:62
  142.5 5.8 %collective-permute-start.35 = (bf16[8,4096]{1,0:T(8,128)(2,1)S(1)}, bf16[8,4096]{1,0:T(8,128)(2,1)S(1)}, u32[]{:S(2)}, u32[]{:S(2)}) collective-permute-start(bf16[8,4096]{1,0:T(8,128)(2,1)S(1)} %fusion.30), channel_id=1, source_target_pairs={{0,8},{16,24},{8,0},{24,16},{1,9},{17,25},{9,1},{25,17},{2,10},{18... | collective-permute-start | bytes 196616 | tf_op jit(solution)/shard_map/ppermute | solution.py:61
  147.5 5.8 %collective-permute-start.41 = (bf16[8,4096]{1,0:T(8,128)(2,1)S(1)}, bf16[8,4096]{1,0:T(8,128)(2,1)S(1)}, u32[]{:S(2)}, u32[]{:S(2)}) collective-permute-start(bf16[8,4096]{1,0:T(8,128)(2,1)S(1)} %fusion.31), channel_id=1, source_target_pairs={{0,64},{32,96},{64,0},{96,32},{1,65},{33,97},{65,1},{97,33},{2,66}... | collective-permute-start | bytes 196616 | tf_op jit(solution)/shard_map/ppermute | solution.py:62
  153.5 4.8 %collective-permute-start.44 = (bf16[2,8192]{1,0:T(2,128)(2,1)S(1)}, bf16[2,8192]{1,0:T(2,128)(2,1)S(1)}, u32[]{:S(2)}, u32[]{:S(2)}) collective-permute-start(bf16[2,8192]{1,0:T(2,128)(2,1)S(1)} %get-tuple-element.60), channel_id=1, source_target_pairs={{0,6},{2,0},{4,2},{6,4},{1,7},{3,1},{5,3},{7,5},{8,14},{10,8},{12,... | collective-permute-start | bytes 98312 | tf_op jit(solution)/shard_map/ppermute | solution.py:26
  156.6 5.1 %collective-permute-start.43 = (bf16[2,8192]{1,0:T(2,128)(2,1)S(1)}, bf16[2,8192]{1,0:T(2,128)(2,1)S(1)}, u32[]{:S(2)}, u32[]{:S(2)}) collective-permute-start(bf16[2,8192]{1,0:T(2,128)(2,1)S(1)} %get-tuple-element.61), channel_id=1, source_target_pairs={{0,2},{2,4},{4,6},{6,0},{1,3},{3,5},{5,7},{7,1},{8,10},{10,12},{12... | collective-permute-start | bytes 98312 | tf_op jit(solution)/shard_map/ppermute | solution.py:26
  156.7 5.5 %collective-permute-start.42 = (bf16[2,8192]{1,0:T(2,128)(2,1)S(1)}, bf16[2,8192]{1,0:T(2,128)(2,1)S(1)}, u32[]{:S(2)}, u32[]{:S(2)}) collective-permute-start(bf16[2,8192]{1,0:T(2,128)(2,1)S(1)} %get-tuple-element.59), channel_id=1, source_target_pairs={{0,4},{2,6},{4,0},{6,2},{1,5},{3,7},{5,1},{7,3},{8,12},{10,14},{12... | collective-permute-start | bytes 98312 | tf_op jit(solution)/shard_map/ppermute | solution.py:26
where the time goes:
time: 164 us; the launch traced here: 163 us
  waiting for transfers between devices  81.1 us (49%)
  starting transfers between devices  52.5 us (32%)
  Pallas kernels  19.4 us (12%)
  other arithmetic  5.24 us (3%)
  local copies, waits for them, and re-layouts  2.69 us (2%)
    ppermute x30, waiting for transfers between devices, shift(): return lax.ppermute(v, ax, [(i, (i + s) % n) for i in range(n)])  49 us
    ppermute x30, starting transfers between devices, shift(): return lax.ppermute(v, ax, [(i, (i + s) % n) for i in range(n)])  36.8 us
    ppermute x6, waiting for transfers between devices, shift(): return lax.ppermute(v, ('xl', 'xh'), [(_x(i), _x(i + s)) for i in range(4)])  16.2 us
    pallas_call x1, Pallas kernels, autoencode(): pl.pallas_call(kernel, in_specs=[SM, VM, VM, VM, VM, HB, VM, VM, VM, VM],...  13.5 us
    ppermute x4, waiting for transfers between devices, swap(): return lax.ppermute(v, ax, [(i, i ^ bit) for i in range(4)])  7.99 us
    ppermute x6, starting transfers between devices, shift(): return lax.ppermute(v, ('xl', 'xh'), [(_x(i), _x(i + s)) for i in range(4)])  7.07 us
    ppermute x4, starting transfers between devices, swap(): lax.ppermute(v, ('xl', 'xh'), [(_x(i), _x(i ^ bit)) for i in range(4)])  6.31 us
    pallas_call x1, Pallas kernels, project(): pl.pallas_call(kernel, in_specs=[SM, HB, HB, HB], out_specs=[VM] * len(co...  5.89 us
  transfers between devices with their start and end apart: 45, of which 23 were waited for; matrix products, arithmetic and copies ran while one was open for 4% of the time, Pallas kernels for 0%

commit v1 on v0

--- a/solution.py
+++ b/solution.py
@@ -87,16 +87,16 @@
     return pltpu.with_memory_space_constraint(v, pltpu.HBM)
 
 
-def project(cols, attn, w_out, resid, counts, dtypes):
+def project(table, skip, place_at, attn, w_out, resid, counts, dtypes):
     rows, inner = attn.shape
     few = resid.shape[0]
     width, steps = 512, sum(counts)
 
-    def kernel(cols_ref, attn_hbm, w_ref, r_hbm, *rest):
+    def kernel(table_ref, attn_hbm, w_ref, r_hbm, *rest):
         outs, (attn_ref, r_ref, buf, sems) = rest[:-4], rest[-4:]
 
         def span(i):
-            return pl.ds(pl.multiple_of(cols_ref[i] * width, width), width)
+            return pl.ds(pl.multiple_of(table_ref[skip + i] * width, width), width)
 
         small = [
             pltpu.make_async_copy(attn_hbm, attn_ref, sems.at[steps]),
@@ -105,7 +105,7 @@
         copies = [pltpu.make_async_copy(w_ref.at[:, span(i)], buf.at[i], sems.at[i]) for i in range(steps)]
         for copy in small + copies:
             copy.start()
-        at = lax.broadcasted_iota(jnp.int32, (rows, few), 0) - cols_ref[3 * steps] * few
+        at = lax.broadcasted_iota(jnp.int32, (rows, few), 0) - table_ref[place_at] * few
         place = jnp.where(at == lax.broadcasted_iota(jnp.int32, (rows, few), 1), 1.0, 0.0).astype(bf16)
         for copy in small:
             copy.wait()
@@ -129,7 +129,7 @@
         ],
         compiler_params=limit(12),
         name="project",
-    )(cols, hbm(attn), hbm(w_out), hbm(resid))
+    )(table, hbm(attn), hbm(w_out), hbm(resid))
 
 
 def autoencode(table, skip, own_a, oth_a, own_b, oth_b, w_enc, b_dec, b_enc, dec_norm, back):
@@ -209,13 +209,15 @@
     y_bits = tuple((b, b ^ 1) for b in (y & 1, y >> 1))
     later += [b for pair in y_bits for b in pair] + [c, c ^ 1, xh, xh ^ 1, xl, xl ^ 1, x, y, z, first]
     homes = [((y - yy) & 3) * 2 + (xl ^ xx) for yy in four for xx in (0, 1)]
-    later += homes
+    base = lat * rows
+    two_own, two_oth = c * 2, (c ^ 1) * 2
+    later += homes + [base, two_own, two_oth]
     table = lax.optimization_barrier(jnp.stack(cols + units + [t] + later))
-    a_send, b2, b1, b3, a_keep, b_keep = project(
-        table, attn_out, w_out, resid_in, (4, 2, 2, 2, 4, 2), (bf16,) * 4 + (f32,) * 2
-    )
+    place_at = len(cols) + len(units)
+    a_send, b2, b1, b3 = project(table, 0, place_at, attn_out, w_out, resid_in, (4, 2, 2, 2), (bf16,) * 4)
     a_got = shift(a_send, "xl", 1)
     b_got = [shift(b2, "y", 2), shift(b1, "y", 1), shift(b3, "y", 3)]
+    a_keep, b_keep = project(table, 10, place_at, attn_out, w_out, resid_in, (4, 2), (f32,) * 2)
     a_more = [shift((a_keep[s] + a_got[s].astype(f32)).astype(bf16), "y", s) for s in (2, 1, 3)]
 
     def b_part(dx):
@@ -228,42 +230,41 @@
     b_sum = b_part(0) + b_more.astype(f32)
     stream = jnp.concatenate([a_sum, b_sum], axis=1).astype(bf16)
 
-    def by_core(v):
-        return v.reshape(4, 2, 2, 4, 2, 2).transpose(4, 0, 2, 1, 3, 5).reshape(2, 128)
-
-    pos2 = by_core(positions)
-    ids = lat * rows + lax.iota(jnp.int32, rows)
-
-    def hot(p):
-        return (p[:, None] == ids[None, :]).astype(bf16)
+    def template_row(r, two_core):
+        xx = (r >> 3) & 3
+        return (r >> 5) * 64 + (xx & 1) * 32 + (xx >> 1) * 16 + ((r >> 1) & 3) * 4 + two_core + (r & 1)
+
+    def iota(shape, axis):
+        return lax.broadcasted_iota(jnp.int32, shape, axis)
+
+    hits = (iota((rows, 256), 0) + base == positions[None, :]).astype(bf16)
+
+    def hot(two_core):
+        rank = (template_row(iota((128, 256), 0), two_core) == iota((128, 256), 1)).astype(bf16)
+        return lax.dot_general(rank, hits, (((1,), (1,)), ((), ())), preferred_element_type=f32).astype(bf16)
 
     def pick(h, s):
         return jnp.dot(h, s, preferred_element_type=f32).astype(bf16)
 
-    hot_own, hot_oth = hot(take(pos2, c)), hot(take(pos2, c ^ 1))
-    parts = stream.reshape(rows, 2, 2, 256)
-    cut_own, cut_oth = (take(parts, i, 2).reshape(rows, 512) for i in (xh, xh ^ 1))
-    both = lax.ppermute(pick(hot_oth, cut_oth), ("xh", "c"), [(i, i ^ 3) for i in range(4)])
-    other_h = shift(pick(hot_own, cut_oth), "xh", 1)
-    other_c = shift(pick(hot_oth, cut_own), "c", 1)
-    v = pick(hot_own, cut_own) + both + other_h + other_c
-    got = [shift(v, "z", s) for s in (2, 1, 3)]
-    v = v + got[0] + got[1] + got[2]
-    s4 = stream.reshape(4, 2, own_rows, 1024)
-    s_got = shift(take(s4, xl ^ 1, 1), "xl", 1)
-    v, s_got = lax.optimization_barrier((v, s_got))
+    v = pick(hot(two_own), stream) + shift(pick(hot(two_oth), stream), "c", 1)
+    v = v.reshape(rows, 2, 2, 256)
+    v = take(v, xh, 2) + shift(take(v, xh ^ 1, 2), "xh", 1)
+    for bit in (1, 2):
+        v = v + swap(v, "z", bit)
     v = v.reshape(rows, 2, 256)
 
     a = gather_double(v[:, 0], "x")
     b = gather_double(v[:, 1], "y")
     a = gather_ring(a, "y")
     b = gather_ring(b, "x")
+    s4 = stream.reshape(4, 2, own_rows, 1024)
+    s_got = shift(take(s4, xl ^ 1, 1), "xl", 1)
+    a, s_got = lax.optimization_barrier((a, s_got))
     a_oth = shift(a, "c", 1)
     b_oth = shift(b, "c", 1)
 
-    idx2 = by_core(lax.iota(jnp.int32, 256))
-    where = jnp.concatenate([take(idx2, c), take(idx2, c ^ 1)])
-    back = (lax.iota(jnp.int32, 256)[:, None] == where[None, :]).astype(bf16)
+    k = iota((256, 256), 1)
+    back = (iota((256, 256), 0) == template_row(k & 127, two_own ^ ((k >> 7) * 2))).astype(bf16)
     codes_out, own_a, oth_a, own_b, oth_b = autoencode(
         table, len(cols), a, a_oth, b, b_oth, w_enc, b_dec, b_enc, dec_norm, back
     )
@@ -282,7 +283,9 @@
     a_s, b_s, _ = lax.optimization_barrier((a, b, own_b))
     s_own = take(s4, xl, 1)
     s_two = jnp.stack([s_own, s_got])
-    s_rel = [take(s_two, y, 1)] + [shift(take(s_two, (y + s) & 3, 1), "y", s) for s in (1, 2, 3)]
+    s_rel = [shift(take(s_two, (y + s) & 3, 1), "y", s) for s in (1, 2, 3)]
+    *s_rel, _ = lax.optimization_barrier((*s_rel, r))
+    s_rel = [take(s_two, y, 1)] + s_rel
     s_rel = jnp.stack(s_rel).reshape(8, own_rows, 1024)
 
     def home(yy, xx, h):

time: 164 us -> 167 us (1.018)
  the two profiles are of different devices: /device:TPU:24 before, /device:TPU:0 now
where the time goes in v1:
time: 167 us
  waiting for transfers between devices  79.4 us (48%)
  starting transfers between devices  59.2 us (35%)
  Pallas kernels  21.2 us (13%)
  other arithmetic  3.19 us (2%)
  local copies, waits for them, and re-layouts  1.81 us (1%)
    ppermute x27, waiting for transfers between devices, shift(): return lax.ppermute(v, ax, [(i, (i + s) % n) for i in range(n)])  42 us
    ppermute x27, starting transfers between devices, shift(): return lax.ppermute(v, ax, [(i, (i + s) % n) for i in range(n)])  32 us
    ppermute x6, waiting for transfers between devices, swap(): return lax.ppermute(v, ax, [(i, i ^ bit) for i in range(4)])  18.6 us
    pallas_call x1, Pallas kernels, autoencode(): pl.pallas_call(kernel, in_specs=[SM, VM, VM, VM, VM, HB, VM, VM, VM, VM],...  13.5 us
    ppermute x6, starting transfers between devices, shift(): return lax.ppermute(v, ('xl', 'xh'), [(_x(i), _x(i + s)) for i in range(4)])  12 us
    ppermute x6, waiting for transfers between devices, shift(): return lax.ppermute(v, ('xl', 'xh'), [(_x(i), _x(i + s)) for i in range(4)])  11.9 us
    pallas_call x2, Pallas kernels, project(): pl.pallas_call(kernel, in_specs=[SM, HB, HB, HB], out_specs=[VM] * len(co...  7.64 us
    ppermute x6, starting transfers between devices, swap(): return lax.ppermute(v, ax, [(i, i ^ bit) for i in range(4)])  7.63 us
  transfers between devices with their start and end apart: 43, of which 27 were waited for; matrix products, arithmetic and copies ran while one was open for 1% of the time, Pallas kernels for 2%

profile of v1, /device:TPU:0, one launch (start us, length us, event | category | flops | bytes accessed | tf_op | source)
XLA Modules:
  0.0 167.2 jit_solution(11503442519721862841)
XLA Ops:
  1.0 4.3 %project.3 = (bf16[4,128,512]{2,1,0:T(8,128)(2,1)S(1)}, bf16[2,128,512]{2,1,0:T(8,128)(2,1)S(1)}, bf16[2,128,512]{2,1,0:T(8,128)(2,1)S(1)}, bf16[2,128,512]{2,1,0:T(8,128)(2,1)S(1)}) custom-call(s32[90]{0:T(128)S(1)} %stack.414.table_ref, bf16[128,512]{1,0:T(8,128)(2,1)} %attn_hbm.3, bf16[512,8192]{1,0:T(8,128)(2,1)} %w_ref.4, bf16[16,8192]{1,0:T(8,128)(2,1)} %r_hbm.3), custom_call_target="tpu_custom_call" | custom-call | tf_op jit(solution)/shard_map/project/pallas_call | solution.py:119
  5.3 1.7 %collective-permute-start = (bf16[4,128,512]{2,1,0:T(8,128)(2,1)S(1)}, bf16[4,128,512]{2,1,0:T(8,128)(2,1)S(1)}, u32[]{:S(2)}, u32[]{:S(2)}) collective-permute-start(bf16[4,128,512]{2,1,0:T(8,128)(2,1)S(1)} %get-tuple-element.23), channel_id=1, source_target_pairs={{0,16},{16,0},{1,17},{17,1},{2,18},{18,2},{3,19},{19,3},{4,20},{20... | collective-permute-start | bytes 1572872 | tf_op jit(solution)/shard_map/ppermute | solution.py:26
  7.0 3.0 %collective-permute-start.6 = (bf16[2,128,512]{2,1,0:T(8,128)(2,1)S(1)}, bf16[2,128,512]{2,1,0:T(8,128)(2,1)S(1)}, u32[]{:S(2)}, u32[]{:S(2)}) collective-permute-start(bf16[2,128,512]{2,1,0:T(8,128)(2,1)S(1)} %get-tuple-element.27), channel_id=1, source_target_pairs={{0,96},{32,0},{64,32},{96,64},{1,97},{33,1},{65,33},{97,65},{2,98}... | collective-permute-start | bytes 786440 | tf_op jit(solution)/shard_map/ppermute | solution.py:26
  10.0 2.2 %collective-permute-start.4 = (bf16[2,128,512]{2,1,0:T(8,128)(2,1)S(1)}, bf16[2,128,512]{2,1,0:T(8,128)(2,1)S(1)}, u32[]{:S(2)}, u32[]{:S(2)}) collective-permute-start(bf16[2,128,512]{2,1,0:T(8,128)(2,1)S(1)} %get-tuple-element.25), channel_id=1, source_target_pairs={{0,64},{32,96},{64,0},{96,32},{1,65},{33,97},{65,1},{97,33},{2,66}... | collective-permute-start | bytes 786440 | tf_op jit(solution)/shard_map/ppermute | solution.py:26
  12.2 3.3 %project.2 = (f32[4,128,512]{2,1,0:T(8,128)S(1)}, f32[2,128,512]{2,1,0:T(8,128)S(1)}) custom-call(s32[90]{0:T(128)S(1)} %stack.414.table_ref, bf16[128,512]{1,0:T(8,128)(2,1)} %attn_hbm.3, bf16[512,8192]{1,0:T(8,128)(2,1)} %w_ref.4, bf16[16,8192]{1,0:T(8,128)(2,1)} %r_hbm.3), custom_call_target="tpu_custom_call" | custom-call | tf_op jit(solution)/shard_map/project/pallas_call | solution.py:119
  15.6 5.4 %collective-permute-done.6 = bf16[2,128,512]{2,1,0:T(8,128)(2,1)S(1)} collective-permute-done((bf16[2,128,512]{2,1,0:T(8,128)(2,1)S(1)}, bf16[2,128,512]{2,1,0:T(8,128)(2,1)S(1)}, u32[]{:S(2)}, u32[]{:S(2)}) %collective-permute-start.6) | collective-permute-done | bytes 262176 | tf_op jit(solution)/shard_map/ppermute | solution.py:26
  20.9 3.4 %collective-permute-done.5 = bf16[2,128,512]{2,1,0:T(8,128)(2,1)S(1)} collective-permute-done((bf16[2,128,512]{2,1,0:T(8,128)(2,1)S(1)}, bf16[2,128,512]{2,1,0:T(8,128)(2,1)S(1)}, u32[]{:S(2)}, u32[]{:S(2)}) %collective-permute-start.5) | collective-permute-done | bytes 262176 | tf_op jit(solution)/shard_map/ppermute | solution.py:26
  24.4 0.6 collective-permute-start.7
  25.2 0.4 collective-permute-start.3
  25.5 1.7 %collective-permute-start.2 = (bf16[128,512]{1,0:T(8,128)(2,1)S(1)}, bf16[128,512]{1,0:T(8,128)(2,1)S(1)}, u32[]{:S(2)}, u32[]{:S(2)}) collective-permute-start(bf16[128,512]{1,0:T(8,128)(2,1)S(1)} %get-tuple-element.44), channel_id=1, source_target_pairs={{0,32},{32,64},{64,96},{96,0},{1,33},{33,65},{65,97},{97,1},{2,34}... | collective-permute-start | bytes 393224 | tf_op jit(solution)/shard_map/ppermute | solution.py:26
  27.3 0.6 collective-permute-start.1
  27.8 1.7 collective-permute-done.7
  29.6 1.3 collective-permute-done.3
  30.8 0.9 collective-permute-done.2
  31.7 2.0 %collective-permute-done.1 = bf16[128,512]{1,0:T(8,128)(2,1)S(1)} collective-permute-done((bf16[128,512]{1,0:T(8,128)(2,1)S(1)}, bf16[128,512]{1,0:T(8,128)(2,1)S(1)}, u32[]{:S(2)}, u32[]{:S(2)}) %collective-permute-start.1) | collective-permute-done | bytes 131104 | tf_op jit(solution)/shard_map/ppermute | solution.py:26
  33.8 0.4 convolution_convert_fusion
  34.4 1.5 collective-permute-done.8
  35.9 0.4 fusion
  36.5 0.5 constant_dynamic-slice_fusion.3
  37.1 3.1 %collective-permute-start.9 = (bf16[128,2,256]{2,0,1:T(8,128)(2,1)S(1)}, bf16[128,2,256]{2,0,1:T(8,128)(2,1)S(1)}, u32[]{:S(2)}, u32[]{:S(2)}) collective-permute-start(bf16[128,2,256]{2,0,1:T(8,128)(2,1)S(1)} %bitcast.295), channel_id=1, source_target_pairs={{0,8},{8,0},{1,9},{9,1},{2,10},{10,2},{3,11},{11,3},{4,12},{12,4},... | collective-permute-start | bytes 393224 | tf_op jit(solution)/shard_map/ppermute | solution.py:26
  40.2 4.0 %collective-permute-done.9 = bf16[128,2,256]{2,0,1:T(8,128)(2,1)S(1)} collective-permute-done((bf16[128,2,256]{2,0,1:T(8,128)(2,1)S(1)}, bf16[128,2,256]{2,0,1:T(8,128)(2,1)S(1)}, u32[]{:S(2)}, u32[]{:S(2)}) %collective-permute-start.9) | collective-permute-done | bytes 131104 | tf_op jit(solution)/shard_map/ppermute | solution.py:26
  44.3 2.0 %collective-permute-start.10 = (bf16[128,2,256]{2,0,1:T(8,128)(2,1)S(1)}, bf16[128,2,256]{2,0,1:T(8,128)(2,1)S(1)}, u32[]{:S(2)}, u32[]{:S(2)}) collective-permute-start(bf16[128,2,256]{2,0,1:T(8,128)(2,1)S(1)} %fusion.24), channel_id=1, source_target_pairs={{0,2},{2,0},{4,6},{6,4},{1,3},{3,1},{5,7},{7,5},{8,10},{10,8},{12,... | collective-permute-start | bytes 393224 | tf_op jit(solution)/shard_map/ppermute | solution.py:62
  46.2 3.1 %collective-permute-done.10 = bf16[128,2,256]{2,0,1:T(8,128)(2,1)S(1)} collective-permute-done((bf16[128,2,256]{2,0,1:T(8,128)(2,1)S(1)}, bf16[128,2,256]{2,0,1:T(8,128)(2,1)S(1)}, u32[]{:S(2)}, u32[]{:S(2)}) %collective-permute-start.10) | collective-permute-done | bytes 131104 | tf_op jit(solution)/shard_map/ppermute | solution.py:62
  49.3 4.0 %collective-permute-start.11 = (bf16[128,2,256]{2,0,1:T(8,128)(2,1)S(1)}, bf16[128,2,256]{2,0,1:T(8,128)(2,1)S(1)}, u32[]{:S(2)}, u32[]{:S(2)}) collective-permute-start(bf16[128,2,256]{2,0,1:T(8,128)(2,1)S(1)} %add.702), channel_id=1, source_target_pairs={{0,4},{2,6},{4,0},{6,2},{1,5},{3,7},{5,1},{7,3},{8,12},{10,14},{12... | collective-permute-start | bytes 393224 | tf_op jit(solution)/shard_map/ppermute | solution.py:62
  53.3 2.9 %collective-permute-done.11 = bf16[128,2,256]{2,0,1:T(8,128)(2,1)S(1)} collective-permute-done((bf16[128,2,256]{2,0,1:T(8,128)(2,1)S(1)}, bf16[128,2,256]{2,0,1:T(8,128)(2,1)S(1)}, u32[]{:S(2)}, u32[]{:S(2)}) %collective-permute-start.11) | collective-permute-done | bytes 131104 | tf_op jit(solution)/shard_map/ppermute | solution.py:62
  56.3 1.5 collective-permute-start.12
  57.9 2.8 %collective-permute-done.12 = bf16[128,256]{1,0:T(8,128)(2,1)S(1)} collective-permute-done((bf16[128,256]{1,0:T(8,128)(2,1)S(1)}, bf16[128,256]{1,0:T(8,128)(2,1)S(1)}, u32[]{:S(2)}, u32[]{:S(2)}) %collective-permute-start.12) | collective-permute-done | bytes 65568 | tf_op jit(solution)/shard_map/ppermute | solution.py:61
  60.7 3.2 %collective-permute-start.13 = (bf16[2,128,256]{2,1,0:T(8,128)(2,1)S(1)}, bf16[2,128,256]{2,1,0:T(8,128)(2,1)S(1)}, u32[]{:S(2)}, u32[]{:S(2)}) collective-permute-start(bf16[2,128,256]{2,1,0:T(8,128)(2,1)S(1)} %pad_maximum_fusion.8), channel_id=1, source_target_pairs={{0,8},{16,24},{8,0},{24,16},{1,9},{17,25},{9,1},{25,17},{2,10},{18... | collective-permute-start | bytes 393224 | tf_op jit(solution)/shard_map/ppermute | solution.py:61
  64.0 3.3 %collective-permute-done.13 = bf16[2,128,256]{2,1,0:T(8,128)(2,1)S(1)} collective-permute-done((bf16[2,128,256]{2,1,0:T(8,128)(2,1)S(1)}, bf16[2,128,256]{2,1,0:T(8,128)(2,1)S(1)}, u32[]{:S(2)}, u32[]{:S(2)}) %collective-permute-start.13) | collective-permute-done | bytes 131104 | tf_op jit(solution)/shard_map/ppermute | solution.py:61
  67.3 1.6 collective-permute-start.16
  68.9 1.5 collective-permute-start.23
  70.4 2.1 %collective-permute-start.15 = (bf16[4,128,256]{2,1,0:T(8,128)(2,1)S(1)}, bf16[4,128,256]{2,1,0:T(8,128)(2,1)S(1)}, u32[]{:S(2)}, u32[]{:S(2)}) collective-permute-start(bf16[4,128,256]{2,1,0:T(8,128)(2,1)S(1)} %get-tuple-element.62), channel_id=1, source_target_pairs={{0,64},{32,96},{64,0},{96,32},{1,65},{33,97},{65,1},{97,33},{2,66}... | collective-permute-start | bytes 786440 | tf_op jit(solution)/shard_map/ppermute | solution.py:26
  72.5 0.5 collective-permute-start.14
  73.0 3.9 %collective-permute-done.23 = bf16[2,128,256]{2,1,0:T(8,128)(2,1)S(1)} collective-permute-done((bf16[2,128,256]{2,1,0:T(8,128)(2,1)S(1)}, bf16[2,128,256]{2,1,0:T(8,128)(2,1)S(1)}, u32[]{:S(2)}, u32[]{:S(2)}) %collective-permute-start.23) | collective-permute-done | bytes 131104 | tf_op jit(solution)/shard_map/ppermute | solution.py:62
  76.9 2.6 %collective-permute-start.26 = (bf16[4,128,256]{2,1,0:T(8,128)(2,1)S(1)}, bf16[4,128,256]{2,1,0:T(8,128)(2,1)S(1)}, u32[]{:S(2)}, u32[]{:S(2)}) collective-permute-start(bf16[4,128,256]{2,1,0:T(8,128)(2,1)S(1)} %get-tuple-element.58), channel_id=1, source_target_pairs={{0,24},{16,0},{8,16},{24,8},{1,25},{17,1},{9,17},{25,9},{2,26},{18... | collective-permute-start | bytes 786440 | tf_op jit(solution)/shard_map/ppermute | solution.py:24
  79.5 1.0 collective-permute-start.25
  80.5 0.7 collective-permute-start.24
  81.3 1.9 %collective-permute-start.17 = (bf16[4,16,1024]{2,1,0:T(8,128)(2,1)S(1)}, bf16[4,16,1024]{2,1,0:T(8,128)(2,1)S(1)}, u32[]{:S(2)}, u32[]{:S(2)}) collective-permute-start(bf16[4,16,1024]{2,1,0:T(8,128)(2,1)S(1)} %get-tuple-element.59), channel_id=1, source_target_pairs={{0,16},{16,0},{1,17},{17,1},{2,18},{18,2},{3,19},{19,3},{4,20},{20... | collective-permute-start | bytes 393224 | tf_op jit(solution)/shard_map/ppermute | solution.py:26
  83.3 5.3 %collective-permute-done.17 = bf16[4,16,1024]{2,1,0:T(8,128)(2,1)S(1)} collective-permute-done((bf16[4,16,1024]{2,1,0:T(8,128)(2,1)S(1)}, bf16[4,16,1024]{2,1,0:T(8,128)(2,1)S(1)}, u32[]{:S(2)}, u32[]{:S(2)}) %collective-permute-start.17) | collective-permute-done | bytes 131104 | tf_op jit(solution)/shard_map/ppermute | solution.py:26
  88.6 1.6 collective-permute-done.24
  90.7 0.6 collective-permute-done.21.ta_ref
  91.3 2.0 %collective-permute-done.27.tb_ref = bf16[4,4,128,256]{3,2,1,0:T(8,128)(2,1)S(1)} collective-permute-done((bf16[4,4,128,256]{3,2,1,0:T(8,128)(2,1)S(1)}, bf16[4,4,128,256]{3,2,1,0:T(8,128)(2,1)S(1)}, u32[]{:S(2)}, u32[]{:S(2)}) %collective-permute-start.27) | collective-permute-done | bytes 1048608 | tf_op jit(solution)/shard_map/ppermute | solution.py:26
  93.3 13.5 %autoencode.1 = (bf16[256,1024]{1,0:T(8,128)(2,1)}, f32[128,4096]{1,0:T(8,128)S(1)}, bf16[128,4096]{1,0:T(8,128)(2,1)S(1)}, f32[128,4096]{1,0:T(8,128)S(1)}, bf16[128,4096]{1,0:T(8,128)(2,1)S(1)}) custom-call(s32[90]{0:T(128)S(1)} %stack.414.table_ref, bf16[4,4,128,256]{3,2,1,0:T(8,128)(2,1)S(1)} %pad_maximum_fusion.oa_ref, ...), custom_call_target="tpu_custom_call" | custom-call | tf_op jit(solution)/shard_map/autoencode/pallas_call | solution.py:175
  107.1 1.6 collective-permute-start.18
  108.7 3.4 %collective-permute-start.19 = (bf16[2,16,1024]{2,1,0:T(8,128)(2,1)S(1)}, bf16[2,16,1024]{2,1,0:T(8,128)(2,1)S(1)}, u32[]{:S(2)}, u32[]{:S(2)}) collective-permute-start(bf16[2,16,1024]{2,1,0:T(8,128)(2,1)S(1)} %get-tuple-element.55), channel_id=1, source_target_pairs={{0,64},{32,96},{64,0},{96,32},{1,65},{33,97},{65,1},{97,33},{2,66}... | collective-permute-start | bytes 196616 | tf_op jit(solution)/shard_map/ppermute | solution.py:26
  112.6 0.7 collective-permute-start.31
  113.3 1.4 collective-permute-start.30
  115.2 6.7 %collective-permute-done.31 = bf16[4,8,4096]{2,1,0:T(8,128)(2,1)S(1)} collective-permute-done((bf16[4,8,4096]{2,1,0:T(8,128)(2,1)S(1)}, bf16[4,8,4096]{2,1,0:T(8,128)(2,1)S(1)}, u32[]{:S(2)}, u32[]{:S(2)}) %collective-permute-start.31) | collective-permute-done | bytes 262176 | tf_op jit(solution)/shard_map/ppermute | solution.py:26
  121.9 3.1 %collective-permute-start.37 = (bf16[4,8,4096]{2,1,0:T(8,128)(2,1)S(1)}, bf16[4,8,4096]{2,1,0:T(8,128)(2,1)S(1)}, u32[]{:S(2)}, u32[]{:S(2)}) collective-permute-start(bf16[4,8,4096]{2,1,0:T(8,128)(2,1)S(1)} %get-tuple-element.46), channel_id=1, source_target_pairs={{0,24},{16,0},{8,16},{24,8},{1,25},{17,1},{9,17},{25,9},{2,26},{18... | collective-permute-start | bytes 786440 | tf_op jit(solution)/shard_map/ppermute | solution.py:24
  125.0 3.3 %collective-permute-done.30 = bf16[4,8,4096]{2,1,0:T(8,128)(2,1)S(1)} collective-permute-done((bf16[4,8,4096]{2,1,0:T(8,128)(2,1)S(1)}, bf16[4,8,4096]{2,1,0:T(8,128)(2,1)S(1)}, u32[]{:S(2)}, u32[]{:S(2)}) %collective-permute-start.30) | collective-permute-done | bytes 262176 | tf_op jit(solution)/shard_map/ppermute | solution.py:26
  128.3 2.0 %collective-permute-start.36 = (bf16[4,8,4096]{2,1,0:T(8,128)(2,1)S(1)}, bf16[4,8,4096]{2,1,0:T(8,128)(2,1)S(1)}, u32[]{:S(2)}, u32[]{:S(2)}) collective-permute-start(bf16[4,8,4096]{2,1,0:T(8,128)(2,1)S(1)} %get-tuple-element.47), channel_id=1, source_target_pairs={{0,16},{16,8},{8,24},{24,0},{1,17},{17,9},{9,25},{25,1},{2,18},{18... | collective-permute-start | bytes 786440 | tf_op jit(solution)/shard_map/ppermute | solution.py:24
  130.3 2.6 %collective-permute-start.35 = (bf16[4,8,4096]{2,1,0:T(8,128)(2,1)S(1)}, bf16[4,8,4096]{2,1,0:T(8,128)(2,1)S(1)}, u32[]{:S(2)}, u32[]{:S(2)}) collective-permute-start(bf16[4,8,4096]{2,1,0:T(8,128)(2,1)S(1)} %get-tuple-element.45), channel_id=1, source_target_pairs={{0,8},{16,24},{8,0},{24,16},{1,9},{17,25},{9,1},{25,17},{2,10},{18... | collective-permute-start | bytes 786440 | tf_op jit(solution)/shard_map/ppermute | solution.py:24
  133.2 4.5 %collective-permute-done.36 = bf16[4,8,4096]{2,1,0:T(8,128)(2,1)S(1)} collective-permute-done((bf16[4,8,4096]{2,1,0:T(8,128)(2,1)S(1)}, bf16[4,8,4096]{2,1,0:T(8,128)(2,1)S(1)}, u32[]{:S(2)}, u32[]{:S(2)}) %collective-permute-start.36) | collective-permute-done | bytes 262176 | tf_op jit(solution)/shard_map/ppermute | solution.py:24
  137.7 1.8 %collective-permute-start.32 = (bf16[2,8,4096]{2,1,0:T(8,128)(2,1)S(1)}, bf16[2,8,4096]{2,1,0:T(8,128)(2,1)S(1)}, u32[]{:S(2)}, u32[]{:S(2)}) collective-permute-start(bf16[2,8,4096]{2,1,0:T(8,128)(2,1)S(1)} %fusion.18), channel_id=1, source_target_pairs={{0,16},{16,0},{8,24},{24,8},{1,17},{17,1},{9,25},{25,9},{2,18},{18... | collective-permute-start | bytes 393224 | tf_op jit(solution)/shard_map/ppermute | solution.py:61
  139.5 5.8 %collective-permute-done.35 = bf16[4,8,4096]{2,1,0:T(8,128)(2,1)S(1)} collective-permute-done((bf16[4,8,4096]{2,1,0:T(8,128)(2,1)S(1)}, bf16[4,8,4096]{2,1,0:T(8,128)(2,1)S(1)}, u32[]{:S(2)}, u32[]{:S(2)}) %collective-permute-start.35) | collective-permute-done | bytes 262176 | tf_op jit(solution)/shard_map/ppermute | solution.py:24
  145.6 1.0 collective-permute-start.33
  146.6 3.9 %collective-permute-done.38 = bf16[2,8,4096]{2,1,0:T(8,128)(2,1)S(1)} collective-permute-done((bf16[2,8,4096]{2,1,0:T(8,128)(2,1)S(1)}, bf16[2,8,4096]{2,1,0:T(8,128)(2,1)S(1)}, u32[]{:S(2)}, u32[]{:S(2)}) %collective-permute-start.38) | collective-permute-done | bytes 131104 | tf_op jit(solution)/shard_map/ppermute | solution.py:62
  150.6 0.8 collective-permute-done.33
  151.6 4.8 %collective-permute-done.39 = bf16[8,4096]{1,0:T(8,128)(2,1)S(1)} collective-permute-done((bf16[8,4096]{1,0:T(8,128)(2,1)S(1)}, bf16[8,4096]{1,0:T(8,128)(2,1)S(1)}, u32[]{:S(2)}, u32[]{:S(2)}) %collective-permute-start.39) | collective-permute-done | bytes 65568 | tf_op jit(solution)/shard_map/ppermute | solution.py:62
  157.0 3.4 %collective-permute-start.42 = (bf16[2,8192]{1,0:T(2,128)(2,1)S(1)}, bf16[2,8192]{1,0:T(2,128)(2,1)S(1)}, u32[]{:S(2)}, u32[]{:S(2)}) collective-permute-start(bf16[2,8192]{1,0:T(2,128)(2,1)S(1)} %get-tuple-element.66), channel_id=1, source_target_pairs={{0,6},{2,0},{4,2},{6,4},{1,7},{3,1},{5,3},{7,5},{8,14},{10,8},{12,... | collective-permute-start | bytes 98312 | tf_op jit(solution)/shard_map/ppermute | solution.py:26
  160.3 1.5 collective-permute-start.40
  161.9 3.5 %collective-permute-done.41 = bf16[2,8192]{1,0:T(2,128)(2,1)S(1)} collective-permute-done((bf16[2,8192]{1,0:T(2,128)(2,1)S(1)}, bf16[2,8192]{1,0:T(2,128)(2,1)S(1)}, u32[]{:S(2)}, u32[]{:S(2)}) %collective-permute-start.41) | collective-permute-done | bytes 32800 | tf_op jit(solution)/shard_map/ppermute | solution.py:26
  165.8 0.8 multiply_reduce_fusion
  166.6 0.5 broadcast_multiply_fusion
  (106 shorter events, 4.7 us)
Async XLA Ops:
  5.3 19.7 %collective-permute-start = (bf16[4,128,512]{2,1,0:T(8,128)(2,1)S(1)}, bf16[4,128,512]{2,1,0:T(8,128)(2,1)S(1)}, u32[]{:S(2)}, u32[]{:S(2)}) collective-permute-start(bf16[4,128,512]{2,1,0:T(8,128)(2,1)S(1)} %get-tuple-element.23), channel_id=1, source_target_pairs={{0,16},{16,0},{1,17},{17,1},{2,18},{18,2},{3,19},{19,3},{4,20},{20... | collective-permute-start | bytes 1572872 | tf_op jit(solution)/shard_map/ppermute | solution.py:26
  7.0 13.9 %collective-permute-start.6 = (bf16[2,128,512]{2,1,0:T(8,128)(2,1)S(1)}, bf16[2,128,512]{2,1,0:T(8,128)(2,1)S(1)}, u32[]{:S(2)}, u32[]{:S(2)}) collective-permute-start(bf16[2,128,512]{2,1,0:T(8,128)(2,1)S(1)} %get-tuple-element.27), channel_id=1, source_target_pairs={{0,96},{32,0},{64,32},{96,64},{1,97},{33,1},{65,33},{97,65},{2,98}... | collective-permute-start | bytes 786440 | tf_op jit(solution)/shard_map/ppermute | solution.py:26
  10.0 14.3 %collective-permute-start.5 = (bf16[2,128,512]{2,1,0:T(8,128)(2,1)S(1)}, bf16[2,128,512]{2,1,0:T(8,128)(2,1)S(1)}, u32[]{:S(2)}, u32[]{:S(2)}) collective-permute-start(bf16[2,128,512]{2,1,0:T(8,128)(2,1)S(1)} %get-tuple-element.26), channel_id=1, source_target_pairs={{0,32},{32,64},{64,96},{96,0},{1,33},{33,65},{65,97},{97,1},{2,34}... | collective-permute-start | bytes 786440 | tf_op jit(solution)/shard_map/ppermute | solution.py:26
  10.0 14.3 %collective-permute-start.4 = (bf16[2,128,512]{2,1,0:T(8,128)(2,1)S(1)}, bf16[2,128,512]{2,1,0:T(8,128)(2,1)S(1)}, u32[]{:S(2)}, u32[]{:S(2)}) collective-permute-start(bf16[2,128,512]{2,1,0:T(8,128)(2,1)S(1)} %get-tuple-element.25), channel_id=1, source_target_pairs={{0,64},{32,96},{64,0},{96,32},{1,65},{33,97},{65,1},{97,33},{2,66}... | collective-permute-start | bytes 786440 | tf_op jit(solution)/shard_map/ppermute | solution.py:26
  24.4 9.4 %copy-start.4 = (s32[256]{0:T(256)S(1)}, s32[256]{0:T(256)}, u32[]{:S(2)}) copy-start(s32[256]{0:T(256)} %param.11) | copy-start | bytes 3076
  24.4 5.0 %collective-permute-start.7 = (bf16[128,512]{1,0:T(8,128)(2,1)S(1)}, bf16[128,512]{1,0:T(8,128)(2,1)S(1)}, u32[]{:S(2)}, u32[]{:S(2)}) collective-permute-start(bf16[128,512]{1,0:T(8,128)(2,1)S(1)} %fusion.17), channel_id=1, source_target_pairs={{0,16},{16,0},{1,17},{17,1},{2,18},{18,2},{3,19},{19,3},{4,20},{20... | collective-permute-start | bytes 393224 | tf_op jit(solution)/shard_map/ppermute | solution.py:26
  25.2 5.7 %collective-permute-start.3 = (bf16[128,512]{1,0:T(8,128)(2,1)S(1)}, bf16[128,512]{1,0:T(8,128)(2,1)S(1)}, u32[]{:S(2)}, u32[]{:S(2)}) collective-permute-start(bf16[128,512]{1,0:T(8,128)(2,1)S(1)} %get-tuple-element.43), channel_id=1, source_target_pairs={{0,96},{32,0},{64,32},{96,64},{1,97},{33,1},{65,33},{97,65},{2,98}... | collective-permute-start | bytes 393224 | tf_op jit(solution)/shard_map/ppermute | solution.py:26
  25.5 6.2 %collective-permute-start.2 = (bf16[128,512]{1,0:T(8,128)(2,1)S(1)}, bf16[128,512]{1,0:T(8,128)(2,1)S(1)}, u32[]{:S(2)}, u32[]{:S(2)}) collective-permute-start(bf16[128,512]{1,0:T(8,128)(2,1)S(1)} %get-tuple-element.44), channel_id=1, source_target_pairs={{0,32},{32,64},{64,96},{96,0},{1,33},{33,65},{65,97},{97,1},{2,34}... | collective-permute-start | bytes 393224 | tf_op jit(solution)/shard_map/ppermute | solution.py:26
  27.3 6.5 %collective-permute-start.1 = (bf16[128,512]{1,0:T(8,128)(2,1)S(1)}, bf16[128,512]{1,0:T(8,128)(2,1)S(1)}, u32[]{:S(2)}, u32[]{:S(2)}) collective-permute-start(bf16[128,512]{1,0:T(8,128)(2,1)S(1)} %get-tuple-element.42), channel_id=1, source_target_pairs={{0,64},{32,96},{64,0},{96,32},{1,65},{33,97},{65,1},{97,33},{2,66}... | collective-permute-start | bytes 393224 | tf_op jit(solution)/shard_map/ppermute | solution.py:26
  34.3 1.6 collective-permute-start.8
  37.1 7.1 %collective-permute-start.9 = (bf16[128,2,256]{2,0,1:T(8,128)(2,1)S(1)}, bf16[128,2,256]{2,0,1:T(8,128)(2,1)S(1)}, u32[]{:S(2)}, u32[]{:S(2)}) collective-permute-start(bf16[128,2,256]{2,0,1:T(8,128)(2,1)S(1)} %bitcast.295), channel_id=1, source_target_pairs={{0,8},{8,0},{1,9},{9,1},{2,10},{10,2},{3,11},{11,3},{4,12},{12,4},... | collective-permute-start | bytes 393224 | tf_op jit(solution)/shard_map/ppermute | solution.py:26
  44.3 5.0 %collective-permute-start.10 = (bf16[128,2,256]{2,0,1:T(8,128)(2,1)S(1)}, bf16[128,2,256]{2,0,1:T(8,128)(2,1)S(1)}, u32[]{:S(2)}, u32[]{:S(2)}) collective-permute-start(bf16[128,2,256]{2,0,1:T(8,128)(2,1)S(1)} %fusion.24), channel_id=1, source_target_pairs={{0,2},{2,0},{4,6},{6,4},{1,3},{3,1},{5,7},{7,5},{8,10},{10,8},{12,... | collective-permute-start | bytes 393224 | tf_op jit(solution)/shard_map/ppermute | solution.py:62
  49.3 6.9 %collective-permute-start.11 = (bf16[128,2,256]{2,0,1:T(8,128)(2,1)S(1)}, bf16[128,2,256]{2,0,1:T(8,128)(2,1)S(1)}, u32[]{:S(2)}, u32[]{:S(2)}) collective-permute-start(bf16[128,2,256]{2,0,1:T(8,128)(2,1)S(1)} %add.702), channel_id=1, source_target_pairs={{0,4},{2,6},{4,0},{6,2},{1,5},{3,7},{5,1},{7,3},{8,12},{10,14},{12... | collective-permute-start | bytes 393224 | tf_op jit(solution)/shard_map/ppermute | solution.py:62
  56.3 4.3 %collective-permute-start.12 = (bf16[128,256]{1,0:T(8,128)(2,1)S(1)}, bf16[128,256]{1,0:T(8,128)(2,1)S(1)}, u32[]{:S(2)}, u32[]{:S(2)}) collective-permute-start(bf16[128,256]{1,0:T(8,128)(2,1)S(1)} %get-tuple-element.69), channel_id=1, source_target_pairs={{0,16},{16,0},{8,24},{24,8},{1,17},{17,1},{9,25},{25,9},{2,18},{18... | collective-permute-start | bytes 196616 | tf_op jit(solution)/shard_map/ppermute | solution.py:61
  60.7 6.6 %collective-permute-start.13 = (bf16[2,128,256]{2,1,0:T(8,128)(2,1)S(1)}, bf16[2,128,256]{2,1,0:T(8,128)(2,1)S(1)}, u32[]{:S(2)}, u32[]{:S(2)}) collective-permute-start(bf16[2,128,256]{2,1,0:T(8,128)(2,1)S(1)} %pad_maximum_fusion.8), channel_id=1, source_target_pairs={{0,8},{16,24},{8,0},{24,16},{1,9},{17,25},{9,1},{25,17},{2,10},{18... | collective-permute-start | bytes 393224 | tf_op jit(solution)/shard_map/ppermute | solution.py:61
  63.9 5.0 %collective-permute-start.22 = (bf16[128,256]{1,0:T(8,128)(2,1)S(1)}, bf16[128,256]{1,0:T(8,128)(2,1)S(1)}, u32[]{:S(2)}, u32[]{:S(2)}) collective-permute-start(bf16[128,256]{1,0:T(8,128)(2,1)S(1)} %get-tuple-element.70), channel_id=1, source_target_pairs={{0,32},{32,0},{64,96},{96,64},{1,33},{33,1},{65,97},{97,65},{2,34}... | collective-permute-start | bytes 196616 | tf_op jit(solution)/shard_map/ppermute | solution.py:62
  67.3 13.2 %collective-permute-start.16 = (bf16[4,128,256]{2,1,0:T(8,128)(2,1)S(1)}, bf16[4,128,256]{2,1,0:T(8,128)(2,1)S(1)}, u32[]{:S(2)}, u32[]{:S(2)}) collective-permute-start(bf16[4,128,256]{2,1,0:T(8,128)(2,1)S(1)} %get-tuple-element.62), channel_id=1, source_target_pairs={{0,96},{32,0},{64,32},{96,64},{1,97},{33,1},{65,33},{97,65},{2,98}... | collective-permute-start | bytes 786440 | tf_op jit(solution)/shard_map/ppermute | solution.py:26
  68.9 8.0 %collective-permute-start.23 = (bf16[2,128,256]{2,1,0:T(8,128)(2,1)S(1)}, bf16[2,128,256]{2,1,0:T(8,128)(2,1)S(1)}, u32[]{:S(2)}, u32[]{:S(2)}) collective-permute-start(bf16[2,128,256]{2,1,0:T(8,128)(2,1)S(1)} %pad_maximum_fusion.9), channel_id=1, source_target_pairs={{0,64},{32,96},{64,0},{96,32},{1,65},{33,97},{65,1},{97,33},{2,66}... | collective-permute-start | bytes 393224 | tf_op jit(solution)/shard_map/ppermute | solution.py:62
  70.4 10.8 %collective-permute-start.15 = (bf16[4,128,256]{2,1,0:T(8,128)(2,1)S(1)}, bf16[4,128,256]{2,1,0:T(8,128)(2,1)S(1)}, u32[]{:S(2)}, u32[]{:S(2)}) collective-permute-start(bf16[4,128,256]{2,1,0:T(8,128)(2,1)S(1)} %get-tuple-element.62), channel_id=1, source_target_pairs={{0,64},{32,96},{64,0},{96,32},{1,65},{33,97},{65,1},{97,33},{2,66}... | collective-permute-start | bytes 786440 | tf_op jit(solution)/shard_map/ppermute | solution.py:26
  72.5 10.7 %collective-permute-start.14 = (bf16[4,128,256]{2,1,0:T(8,128)(2,1)S(1)}, bf16[4,128,256]{2,1,0:T(8,128)(2,1)S(1)}, u32[]{:S(2)}, u32[]{:S(2)}) collective-permute-start(bf16[4,128,256]{2,1,0:T(8,128)(2,1)S(1)} %get-tuple-element.62), channel_id=1, source_target_pairs={{0,32},{32,64},{64,96},{96,0},{1,33},{33,65},{65,97},{97,1},{2,34}... | collective-permute-start | bytes 786440 | tf_op jit(solution)/shard_map/ppermute | solution.py:26
  76.9 11.7 %collective-permute-start.26 = (bf16[4,128,256]{2,1,0:T(8,128)(2,1)S(1)}, bf16[4,128,256]{2,1,0:T(8,128)(2,1)S(1)}, u32[]{:S(2)}, u32[]{:S(2)}) collective-permute-start(bf16[4,128,256]{2,1,0:T(8,128)(2,1)S(1)} %get-tuple-element.58), channel_id=1, source_target_pairs={{0,24},{16,0},{8,16},{24,8},{1,25},{17,1},{9,17},{25,9},{2,26},{18... | collective-permute-start | bytes 786440 | tf_op jit(solution)/shard_map/ppermute | solution.py:24
  79.5 9.1 %collective-permute-start.25 = (bf16[4,128,256]{2,1,0:T(8,128)(2,1)S(1)}, bf16[4,128,256]{2,1,0:T(8,128)(2,1)S(1)}, u32[]{:S(2)}, u32[]{:S(2)}) collective-permute-start(bf16[4,128,256]{2,1,0:T(8,128)(2,1)S(1)} %get-tuple-element.58), channel_id=1, source_target_pairs={{0,8},{16,24},{8,0},{24,16},{1,9},{17,25},{9,1},{25,17},{2,10},{18... | collective-permute-start | bytes 786440 | tf_op jit(solution)/shard_map/ppermute | solution.py:24
  80.5 9.7 %collective-permute-start.24 = (bf16[4,128,256]{2,1,0:T(8,128)(2,1)S(1)}, bf16[4,128,256]{2,1,0:T(8,128)(2,1)S(1)}, u32[]{:S(2)}, u32[]{:S(2)}) collective-permute-start(bf16[4,128,256]{2,1,0:T(8,128)(2,1)S(1)} %get-tuple-element.58), channel_id=1, source_target_pairs={{0,16},{16,8},{8,24},{24,0},{1,17},{17,9},{9,25},{25,1},{2,18},{18... | collective-permute-start | bytes 786440 | tf_op jit(solution)/shard_map/ppermute | solution.py:24
  81.3 7.3 %collective-permute-start.17 = (bf16[4,16,1024]{2,1,0:T(8,128)(2,1)S(1)}, bf16[4,16,1024]{2,1,0:T(8,128)(2,1)S(1)}, u32[]{:S(2)}, u32[]{:S(2)}) collective-permute-start(bf16[4,16,1024]{2,1,0:T(8,128)(2,1)S(1)} %get-tuple-element.59), channel_id=1, source_target_pairs={{0,16},{16,0},{1,17},{17,1},{2,18},{18,2},{3,19},{19,3},{4,20},{20... | collective-permute-start | bytes 393224 | tf_op jit(solution)/shard_map/ppermute | solution.py:26
  83.2 10.1 %copy-start = (f32[8192]{0:T(1024)S(1)}, f32[8192]{0:T(1024)}, u32[]{:S(2)}) copy-start(f32[8192]{0:T(1024)} %param.15) | copy-start | bytes 98308
  83.2 10.1 %copy-start.1 = (f32[1024]{0:T(1024)S(1)}, f32[1024]{0:T(1024)}, u32[]{:S(2)}) copy-start(f32[1024]{0:T(1024)} %param.13) | copy-start | bytes 12292
  83.2 10.1 %copy-start.2 = (f32[1024]{0:T(1024)S(1)}, f32[1024]{0:T(1024)}, u32[]{:S(2)}) copy-start(f32[1024]{0:T(1024)} %param.14) | copy-start | bytes 12292
  88.6 2.7 %collective-permute-start.21 = (bf16[4,4,128,256]{3,2,1,0:T(8,128)(2,1)S(1)}, bf16[4,4,128,256]{3,2,1,0:T(8,128)(2,1)S(1)}, u32[]{:S(2)}, u32[]{:S(2)}) collective-permute-start(bf16[4,4,128,256]{3,2,1,0:T(8,128)(2,1)S(1)} %pad_maximum_fusion.oa_ref), channel_id=1, source_target_pairs={{0,1},{1,0},{2,3},{3,2},{4,5},{5,4},{6,7},{7,6},{8,9},{9,8},{10,11... | collective-permute-start | bytes 3145736 | tf_op jit(solution)/shard_map/ppermute | solution.py:26
  90.3 2.9 %collective-permute-start.27 = (bf16[4,4,128,256]{3,2,1,0:T(8,128)(2,1)S(1)}, bf16[4,4,128,256]{3,2,1,0:T(8,128)(2,1)S(1)}, u32[]{:S(2)}, u32[]{:S(2)}) collective-permute-start(bf16[4,4,128,256]{3,2,1,0:T(8,128)(2,1)S(1)} %pad_maximum_fusion.1.ob_ref), channel_id=1, source_target_pairs={{0,1},{1,0},{2,3},{3,2},{4,5},{5,4},{6,7},{7,6},{8,9},{9,8},{10,11... | collective-permute-start | bytes 3145736 | tf_op jit(solution)/shard_map/ppermute | solution.py:26
  106.8 5.5 %collective-permute-start.28 = (bf16[128,4096]{1,0:T(8,128)(2,1)S(1)}, bf16[128,4096]{1,0:T(8,128)(2,1)S(1)}, u32[]{:S(2)}, u32[]{:S(2)}) collective-permute-start(bf16[128,4096]{1,0:T(8,128)(2,1)S(1)} %get-tuple-element.31), channel_id=1, source_target_pairs={{0,1},{1,0},{2,3},{3,2},{4,5},{5,4},{6,7},{7,6},{8,9},{9,8},{10,11... | collective-permute-start | bytes 3145736 | tf_op jit(solution)/shard_map/ppermute | solution.py:26
  107.1 49.5 %collective-permute-start.18 = (bf16[2,16,1024]{2,1,0:T(8,128)(2,1)S(1)}, bf16[2,16,1024]{2,1,0:T(8,128)(2,1)S(1)}, u32[]{:S(2)}, u32[]{:S(2)}) collective-permute-start(bf16[2,16,1024]{2,1,0:T(8,128)(2,1)S(1)} %get-tuple-element.54), channel_id=1, source_target_pairs={{0,32},{32,64},{64,96},{96,0},{1,33},{33,65},{65,97},{97,1},{2,34}... | collective-permute-start | bytes 196616 | tf_op jit(solution)/shard_map/ppermute | solution.py:26
  108.7 47.9 %collective-permute-start.19 = (bf16[2,16,1024]{2,1,0:T(8,128)(2,1)S(1)}, bf16[2,16,1024]{2,1,0:T(8,128)(2,1)S(1)}, u32[]{:S(2)}, u32[]{:S(2)}) collective-permute-start(bf16[2,16,1024]{2,1,0:T(8,128)(2,1)S(1)} %get-tuple-element.55), channel_id=1, source_target_pairs={{0,64},{32,96},{64,0},{96,32},{1,65},{33,97},{65,1},{97,33},{2,66}... | collective-permute-start | bytes 196616 | tf_op jit(solution)/shard_map/ppermute | solution.py:26
  112.0 2.7 %collective-permute-start.34 = (bf16[128,4096]{1,0:T(8,128)(2,1)S(1)}, bf16[128,4096]{1,0:T(8,128)(2,1)S(1)}, u32[]{:S(2)}, u32[]{:S(2)}) collective-permute-start(bf16[128,4096]{1,0:T(8,128)(2,1)S(1)} %get-tuple-element.33), channel_id=1, source_target_pairs={{0,1},{1,0},{2,3},{3,2},{4,5},{5,4},{6,7},{7,6},{8,9},{9,8},{10,11... | collective-permute-start | bytes 3145736 | tf_op jit(solution)/shard_map/ppermute | solution.py:26
  112.6 9.2 %collective-permute-start.31 = (bf16[4,8,4096]{2,1,0:T(8,128)(2,1)S(1)}, bf16[4,8,4096]{2,1,0:T(8,128)(2,1)S(1)}, u32[]{:S(2)}, u32[]{:S(2)}) collective-permute-start(bf16[4,8,4096]{2,1,0:T(8,128)(2,1)S(1)} %get-tuple-element.49), channel_id=1, source_target_pairs={{0,96},{32,0},{64,32},{96,64},{1,97},{33,1},{65,33},{97,65},{2,98}... | collective-permute-start | bytes 786440 | tf_op jit(solution)/shard_map/ppermute | solution.py:26
  113.3 15.0 %collective-permute-start.30 = (bf16[4,8,4096]{2,1,0:T(8,128)(2,1)S(1)}, bf16[4,8,4096]{2,1,0:T(8,128)(2,1)S(1)}, u32[]{:S(2)}, u32[]{:S(2)}) collective-permute-start(bf16[4,8,4096]{2,1,0:T(8,128)(2,1)S(1)} %get-tuple-element.50), channel_id=1, source_target_pairs={{0,32},{32,64},{64,96},{96,0},{1,33},{33,65},{65,97},{97,1},{2,34}... | collective-permute-start | bytes 786440 | tf_op jit(solution)/shard_map/ppermute | solution.py:26
  114.7 15.6 %collective-permute-start.29 = (bf16[4,8,4096]{2,1,0:T(8,128)(2,1)S(1)}, bf16[4,8,4096]{2,1,0:T(8,128)(2,1)S(1)}, u32[]{:S(2)}, u32[]{:S(2)}) collective-permute-start(bf16[4,8,4096]{2,1,0:T(8,128)(2,1)S(1)} %get-tuple-element.48), channel_id=1, source_target_pairs={{0,64},{32,96},{64,0},{96,32},{1,65},{33,97},{65,1},{97,33},{2,66}... | collective-permute-start | bytes 786440 | tf_op jit(solution)/shard_map/ppermute | solution.py:26
  121.9 11.2 %collective-permute-start.37 = (bf16[4,8,4096]{2,1,0:T(8,128)(2,1)S(1)}, bf16[4,8,4096]{2,1,0:T(8,128)(2,1)S(1)}, u32[]{:S(2)}, u32[]{:S(2)}) collective-permute-start(bf16[4,8,4096]{2,1,0:T(8,128)(2,1)S(1)} %get-tuple-element.46), channel_id=1, source_target_pairs={{0,24},{16,0},{8,16},{24,8},{1,25},{17,1},{9,17},{25,9},{2,26},{18... | collective-permute-start | bytes 786440 | tf_op jit(solution)/shard_map/ppermute | solution.py:24
  128.3 9.4 %collective-permute-start.36 = (bf16[4,8,4096]{2,1,0:T(8,128)(2,1)S(1)}, bf16[4,8,4096]{2,1,0:T(8,128)(2,1)S(1)}, u32[]{:S(2)}, u32[]{:S(2)}) collective-permute-start(bf16[4,8,4096]{2,1,0:T(8,128)(2,1)S(1)} %get-tuple-element.47), channel_id=1, source_target_pairs={{0,16},{16,8},{8,24},{24,0},{1,17},{17,9},{9,25},{25,1},{2,18},{18... | collective-permute-start | bytes 786440 | tf_op jit(solution)/shard_map/ppermute | solution.py:24
  130.3 14.9 %collective-permute-start.35 = (bf16[4,8,4096]{2,1,0:T(8,128)(2,1)S(1)}, bf16[4,8,4096]{2,1,0:T(8,128)(2,1)S(1)}, u32[]{:S(2)}, u32[]{:S(2)}) collective-permute-start(bf16[4,8,4096]{2,1,0:T(8,128)(2,1)S(1)} %get-tuple-element.45), channel_id=1, source_target_pairs={{0,8},{16,24},{8,0},{24,16},{1,9},{17,25},{9,1},{25,17},{2,10},{18... | collective-permute-start | bytes 786440 | tf_op jit(solution)/shard_map/ppermute | solution.py:24
  133.1 23.5 %collective-permute-start.20 = (bf16[2,16,1024]{2,1,0:T(8,128)(2,1)S(1)}, bf16[2,16,1024]{2,1,0:T(8,128)(2,1)S(1)}, u32[]{:S(2)}, u32[]{:S(2)}) collective-permute-start(bf16[2,16,1024]{2,1,0:T(8,128)(2,1)S(1)} %get-tuple-element.56), channel_id=1, source_target_pairs={{0,96},{32,0},{64,32},{96,64},{1,97},{33,1},{65,33},{97,65},{2,98}... | collective-permute-start | bytes 196616 | tf_op jit(solution)/shard_map/ppermute | solution.py:26
  137.7 7.8 %collective-permute-start.32 = (bf16[2,8,4096]{2,1,0:T(8,128)(2,1)S(1)}, bf16[2,8,4096]{2,1,0:T(8,128)(2,1)S(1)}, u32[]{:S(2)}, u32[]{:S(2)}) collective-permute-start(bf16[2,8,4096]{2,1,0:T(8,128)(2,1)S(1)} %fusion.18), channel_id=1, source_target_pairs={{0,16},{16,0},{8,24},{24,8},{1,17},{17,1},{9,25},{25,9},{2,18},{18... | collective-permute-start | bytes 393224 | tf_op jit(solution)/shard_map/ppermute | solution.py:61
  145.4 5.0 %collective-permute-start.38 = (bf16[2,8,4096]{2,1,0:T(8,128)(2,1)S(1)}, bf16[2,8,4096]{2,1,0:T(8,128)(2,1)S(1)}, u32[]{:S(2)}, u32[]{:S(2)}) collective-permute-start(bf16[2,8,4096]{2,1,0:T(8,128)(2,1)S(1)} %fusion.19), channel_id=1, source_target_pairs={{0,32},{32,0},{64,96},{96,64},{1,33},{33,1},{65,97},{97,65},{2,34}... | collective-permute-start | bytes 393224 | tf_op jit(solution)/shard_map/ppermute | solution.py:62
  145.6 5.8 %collective-permute-start.33 = (bf16[8,4096]{1,0:T(8,128)(2,1)S(1)}, bf16[8,4096]{1,0:T(8,128)(2,1)S(1)}, u32[]{:S(2)}, u32[]{:S(2)}) collective-permute-start(bf16[8,4096]{1,0:T(8,128)(2,1)S(1)} %fusion.27), channel_id=1, source_target_pairs={{0,8},{16,24},{8,0},{24,16},{1,9},{17,25},{9,1},{25,17},{2,10},{18... | collective-permute-start | bytes 196616 | tf_op jit(solution)/shard_map/ppermute | solution.py:61
  150.5 5.8 %collective-permute-start.39 = (bf16[8,4096]{1,0:T(8,128)(2,1)S(1)}, bf16[8,4096]{1,0:T(8,128)(2,1)S(1)}, u32[]{:S(2)}, u32[]{:S(2)}) collective-permute-start(bf16[8,4096]{1,0:T(8,128)(2,1)S(1)} %fusion.28), channel_id=1, source_target_pairs={{0,64},{32,96},{64,0},{96,32},{1,65},{33,97},{65,1},{97,33},{2,66}... | collective-permute-start | bytes 196616 | tf_op jit(solution)/shard_map/ppermute | solution.py:62
  157.0 5.0 %collective-permute-start.42 = (bf16[2,8192]{1,0:T(2,128)(2,1)S(1)}, bf16[2,8192]{1,0:T(2,128)(2,1)S(1)}, u32[]{:S(2)}, u32[]{:S(2)}) collective-permute-start(bf16[2,8192]{1,0:T(2,128)(2,1)S(1)} %get-tuple-element.66), channel_id=1, source_target_pairs={{0,6},{2,0},{4,2},{6,4},{1,7},{3,1},{5,3},{7,5},{8,14},{10,8},{12,... | collective-permute-start | bytes 98312 | tf_op jit(solution)/shard_map/ppermute | solution.py:26
  160.3 5.1 %collective-permute-start.41 = (bf16[2,8192]{1,0:T(2,128)(2,1)S(1)}, bf16[2,8192]{1,0:T(2,128)(2,1)S(1)}, u32[]{:S(2)}, u32[]{:S(2)}) collective-permute-start(bf16[2,8192]{1,0:T(2,128)(2,1)S(1)} %get-tuple-element.67), channel_id=1, source_target_pairs={{0,2},{2,4},{4,6},{6,0},{1,3},{3,5},{5,7},{7,1},{8,10},{10,12},{12... | collective-permute-start | bytes 98312 | tf_op jit(solution)/shard_map/ppermute | solution.py:26
  160.3 5.5 %collective-permute-start.40 = (bf16[2,8192]{1,0:T(2,128)(2,1)S(1)}, bf16[2,8192]{1,0:T(2,128)(2,1)S(1)}, u32[]{:S(2)}, u32[]{:S(2)}) collective-permute-start(bf16[2,8192]{1,0:T(2,128)(2,1)S(1)} %get-tuple-element.65), channel_id=1, source_target_pairs={{0,4},{2,6},{4,0},{6,2},{1,5},{3,7},{5,1},{7,3},{8,12},{10,14},{12... | collective-permute-start | bytes 98312 | tf_op jit(solution)/shard_map/ppermute | solution.py:26
  161.9 5.3 %copy-start.3 = (bf16[16,8192]{1,0:T(8,128)(2,1)}, bf16[16,8192]{1,0:T(8,128)(2,1)S(1)}, u32[]{:S(2)}) copy-start(bf16[16,8192]{1,0:T(8,128)(2,1)S(1)} %constant_dynamic-update-slice_fusion.2) | copy-start | bytes 786436

commit v2 on v1

--- a/solution.py
+++ b/solution.py
@@ -53,7 +53,7 @@
 
 def gather_ring(v, ax):
     got = {s: shift(v, ax, s) for s in (2, 1, 3)}
-    return jnp.stack([v, got[1], got[2], got[3]])
+    return jnp.stack([got[1], got[2], got[3]])
 
 
 def swap(v, ax, bit):
@@ -132,55 +132,123 @@
     )(table, hbm(attn), hbm(w_out), hbm(resid))
 
 
-def autoencode(table, skip, own_a, oth_a, own_b, oth_b, w_enc, b_dec, b_enc, dec_norm, back):
+def add_terms(total, table_ref, bd_ref, buf, copies, slots):
+    for (own, oth, j, rows), copy in zip(slots, copies):
+        lhs = jnp.concatenate([own(), oth()], axis=0)
+        lhs = (lhs.astype(f32) - bd_ref[table_ref[j]]).astype(bf16)
+        copy.wait()
+        term = jnp.dot(lhs, buf[rows], preferred_element_type=f32)
+        total = term if total is None else total + term
+    return total
+
+
+def first_terms(table, skip, own, oth, w_enc, b_dec):
+    half, width = own.shape[2:]
+    lat = w_enc.shape[1]
+    n = 8
+
+    def kernel(table_ref, own_ref, oth_ref, w_ref, bd_ref, out_ref, buf, sems):
+        slots, copies = [], []
+        for i in range(n):
+            h, k = i // 4, i % 4
+            j = skip + 16 * h + k
+            rows = pl.ds(pl.multiple_of(table_ref[j] * width, width), width)
+            copies.append(pltpu.make_async_copy(w_ref.at[rows], buf.at[pl.ds(i * width, width)], sems.at[i]))
+            slots.append((lambda h=h, k=k: own_ref[h, k], lambda h=h, k=k: oth_ref[h, k], j, pl.ds(i * width, width)))
+        for copy in copies:
+            copy.start()
+        out_ref[...] = add_terms(None, table_ref, bd_ref, buf, copies, slots)
+
+    return pl.pallas_call(
+        kernel,
+        in_specs=[SM, VM, VM, HB, VM],
+        out_specs=VM,
+        out_shape=jax.ShapeDtypeStruct((2 * half, lat), f32),
+        scratch_shapes=[pltpu.VMEM((n * width, lat), bf16), pltpu.SemaphoreType.DMA((n,))],
+        compiler_params=limit(12),
+        name="first_terms",
+    )(table, own, oth, hbm(w_enc), b_dec.reshape(-1, 1, width))
+
+
+def decode_half(codes, w_ref, own_ref, oth_ref, half):
+    width = 512
+    for i in range(w_ref.shape[0] // width):
+        at = slice(i * width, (i + 1) * width)
+        r = lax.dot_general(codes, w_ref[at], (((1,), (1,)), ((), ())), preferred_element_type=f32)
+        own_ref[:, at] = r[:half]
+        oth_ref[:, at] = r[half:].astype(bf16)
+
+
+def autoencode(table, skip, acc, own_a, oth_a, own_b, oth_b, w_enc, b_dec, b_enc, dec_norm, back):
     half, width = own_a.shape[2:]
     d_model, lat = w_enc.shape
     n = d_model // width
     per = n // 2
     split = d_model // 2
-    out_width = 512
-
-    def kernel(table_ref, oa_ref, ta_ref, ob_ref, tb_ref, w_ref, bd_ref, be_ref, dn_ref, back_ref, codes_ref, *rest):
-        outs, (buf, sems) = rest[:4], rest[4:]
-
-        def span(j):
-            return pl.ds(pl.multiple_of(table_ref[skip + j] * width, width), width)
-
-        copies = [pltpu.make_async_copy(w_ref.at[span(j)], buf.at[span(j)], sems.at[j]) for j in range(n)]
-        for copy in copies:
-            copy.start()
-        total = None
-        for h, (o_ref, t_ref) in enumerate(((oa_ref, ta_ref), (ob_ref, tb_ref))):
-            for j in range(h * per, (h + 1) * per):
-                i, k = j // 4 % 4, j % 4
-                lhs = jnp.concatenate([o_ref[i, k], t_ref[i, k]], axis=0)
-                lhs = (lhs.astype(f32) - bd_ref[table_ref[skip + j]]).astype(bf16)
-                copies[j].wait()
-                term = jnp.dot(lhs, buf[span(j)], preferred_element_type=f32)
-                total = term if total is None else total + term
+
+    def kernel(table_ref, acc_ref, oa_ref, ta_ref, ob_ref, tb_ref, w_ref, bd_ref, be_ref, dn_ref, back_ref, *rest):
+        codes_ref, sorted_ref, own_ref, oth_ref, hi_ref, lo_ref, sems = rest
+
+        def fetch(j):
+            h = j // per
+            unit = table_ref[skip + j]
+            local = pl.ds(pl.multiple_of((unit - h * per) * width, width), width)
+            rows = pl.ds(pl.multiple_of(unit * width, width), width)
+            return pltpu.make_async_copy(w_ref.at[rows], (lo_ref, hi_ref)[h].at[local], sems.at[j]), local
+
+        order = [h * per + j for h in range(2) for j in range(4, per)]
+        order += [h * per + j for h in range(2) for j in range(4)]
+        made = {j: fetch(j) for j in order}
+        for j in order:
+            made[j][0].start()
+        total = acc_ref[...]
+        for h, (o_ref, t_ref, buf) in enumerate(((oa_ref, ta_ref, lo_ref), (ob_ref, tb_ref, hi_ref))):
+            mine = range(h * per + 4, (h + 1) * per)
+            slots = []
+            for j in mine:
+                i, k = j // 4 % 4 - 1, j % 4
+                slots.append((lambda o=o_ref, i=i, k=k: o[i, k], lambda t=t_ref, i=i, k=k: t[i, k], skip + j, made[j][1]))
+            total = add_terms(total, table_ref, bd_ref, buf, [made[j][0] for j in mine], slots)
+        for j in order[-8:]:
+            made[j][0].wait()
         pre = total + be_ref[...]
         codes = (jnp.maximum(pre, 0.0) * dn_ref[...]).astype(bf16)
-        codes_ref[...] = jnp.dot(back_ref[...], codes, preferred_element_type=f32).astype(bf16)
-        for i in range(d_model // out_width):
-            own_ref, oth_ref = outs[:2] if i * out_width < split else outs[2:]
-            first = i * out_width % split
-            to = slice(first, first + out_width)
-            w = buf[i * out_width : (i + 1) * out_width]
-            r = lax.dot_general(codes, w, (((1,), (1,)), ((), ())), preferred_element_type=f32)
-            own_ref[:, to] = r[:half]
-            oth_ref[:, to] = r[half:].astype(bf16)
-
-    own_shape = jax.ShapeDtypeStruct((half, split), f32)
-    oth_shape = jax.ShapeDtypeStruct((half, split), bf16)
+        codes_ref[...] = codes
+        sorted_ref[...] = jnp.dot(back_ref[...], codes, preferred_element_type=f32).astype(bf16)
+        decode_half(codes, lo_ref, own_ref, oth_ref, half)
+
+    codes_shape = jax.ShapeDtypeStruct((2 * half, lat), bf16)
     return pl.pallas_call(
         kernel,
-        in_specs=[SM, VM, VM, VM, VM, HB, VM, VM, VM, VM],
+        in_specs=[SM, VM, VM, VM, VM, VM, HB, VM, VM, VM, VM],
         out_specs=[VM] * 5,
-        out_shape=[jax.ShapeDtypeStruct((2 * half, lat), bf16), own_shape, oth_shape, own_shape, oth_shape],
-        scratch_shapes=[pltpu.VMEM((d_model, lat), bf16), pltpu.SemaphoreType.DMA((n,))],
-        compiler_params=limit(22),
+        out_shape=[
+            codes_shape,
+            codes_shape,
+            jax.ShapeDtypeStruct((half, split), f32),
+            jax.ShapeDtypeStruct((half, split), bf16),
+            jax.ShapeDtypeStruct((split, lat), bf16),
+        ],
+        scratch_shapes=[pltpu.VMEM((split, lat), bf16), pltpu.SemaphoreType.DMA((n,))],
+        compiler_params=limit(20),
         name="autoencode",
-    )(table, own_a, oth_a, own_b, oth_b, hbm(w_enc), b_dec.reshape(-1, 1, width), b_enc[None], dec_norm[None], back)
+    )(table, acc, own_a, oth_a, own_b, oth_b, hbm(w_enc), b_dec.reshape(-1, 1, width), b_enc[None], dec_norm[None], back)
+
+
+def decode(codes, w):
+    half, n = codes.shape[0] // 2, w.shape[0]
+
+    def kernel(codes_ref, w_ref, own_ref, oth_ref):
+        decode_half(codes_ref[...], w_ref, own_ref, oth_ref, half)
+
+    return pl.pallas_call(
+        kernel,
+        in_specs=[VM, VM],
+        out_specs=[VM, VM],
+        out_shape=[jax.ShapeDtypeStruct((half, n), f32), jax.ShapeDtypeStruct((half, n), bf16)],
+        compiler_params=limit(8),
+        name="decode",
+    )(codes, w)
 
 
 def step(attn_out, w_out, resid_in, positions, w_enc, b_enc, dec_norm, b_dec):
@@ -212,7 +280,9 @@
     base = lat * rows
     two_own, two_oth = c * 2, (c ^ 1) * 2
     later += homes + [base, two_own, two_oth]
-    table = lax.optimization_barrier(jnp.stack(cols + units + [t] + later))
+    places_at = len(cols) + len(units) + 1
+    placed = units[:4] + units[16:20] + units[4:16] + units[20:]
+    table = lax.optimization_barrier(jnp.stack(cols + units + [t] + placed + later))
     place_at = len(cols) + len(units)
     a_send, b2, b1, b3 = project(table, 0, place_at, attn_out, w_out, resid_in, (4, 2, 2, 2), (bf16,) * 4)
     a_got = shift(a_send, "xl", 1)
@@ -255,20 +325,23 @@
 
     a = gather_double(v[:, 0], "x")
     b = gather_double(v[:, 1], "y")
-    a = gather_ring(a, "y")
-    b = gather_ring(b, "x")
+    near = jnp.stack([a, b])
+    near_oth = shift(near, "c", 1)
+    acc = first_terms(table, len(cols), near, near_oth, w_enc, b_dec)
+    a_far = gather_ring(a, "y")
+    b_far = gather_ring(b, "x")
+    a_oth = shift(a_far, "c", 1)
+    b_oth = shift(b_far, "c", 1)
     s4 = stream.reshape(4, 2, own_rows, 1024)
     s_got = shift(take(s4, xl ^ 1, 1), "xl", 1)
-    a, s_got = lax.optimization_barrier((a, s_got))
-    a_oth = shift(a, "c", 1)
-    b_oth = shift(b, "c", 1)
 
     k = iota((256, 256), 1)
     back = (iota((256, 256), 0) == template_row(k & 127, two_own ^ ((k >> 7) * 2))).astype(bf16)
-    codes_out, own_a, oth_a, own_b, oth_b = autoencode(
-        table, len(cols), a, a_oth, b, b_oth, w_enc, b_dec, b_enc, dec_norm, back
+    codes, codes_out, own_a, oth_a, w_hi = autoencode(
+        table, len(cols), acc, a_far, a_oth, b_far, b_oth, w_enc, b_dec, b_enc, dec_norm, back
     )
     got_a = shift(oth_a, "c", 1)
+    own_b, oth_b = decode(codes, w_hi)
     got_b = shift(oth_b, "c", 1)
 
     h_a = (own_a + got_a.astype(f32)).astype(bf16).reshape(4, 4, 8, 4096)
@@ -280,7 +353,7 @@
     r = jnp.concatenate([r_a, r_b], axis=1).astype(bf16).reshape(4, 2, 8192)
     full = reduce_ring(r, "z") + b_dec
 
-    a_s, b_s, _ = lax.optimization_barrier((a, b, own_b))
+    near_s, a_s, b_s, _ = lax.optimization_barrier((near, a_far, b_far, own_b))
     s_own = take(s4, xl, 1)
     s_two = jnp.stack([s_own, s_got])
     s_rel = [shift(take(s_two, (y + s) & 3, 1), "y", s) for s in (1, 2, 3)]
@@ -295,9 +368,9 @@
     pieces += [home(yy, xx, 1) for xx in (0, 1) for yy in four]
     stream_out = jnp.concatenate(pieces, axis=1)
 
-    mine_a, mine_b = (cut(v.reshape(16, 128, 256), (0, first, 0), (16, 2, 256)) for v in (a_s, b_s))
-    mine = jnp.concatenate([mine_a, mine_b])
-    places = table[len(cols) : len(cols) + 32]
+    mine = [cut(v.reshape(-1, 128, 256), (0, first, 0), (n, 2, 256)) for v, n in ((near_s, 8), (a_s, 12), (b_s, 12))]
+    mine = jnp.concatenate(mine)
+    places = table[places_at : places_at + 32]
     unsort = (lax.iota(jnp.int32, 32)[:, None] == places[None, :]).astype(bf16)
     mine = jnp.dot(unsort, mine.reshape(32, 512), preferred_element_type=f32)
     mine = mine.reshape(32, 2, 256).transpose(1, 0, 2).reshape(2, 8192)

time: 167 us -> 174 us (1.042)
  the two profiles are of different devices: /device:TPU:0 before, /device:TPU:2 now
where the time goes in v2:
time: 174 us; the launch traced here: 173 us
  waiting for transfers between devices  81 us (47%)
  starting transfers between devices  61.7 us (35%)
  Pallas kernels  23.3 us (13%)
  other arithmetic  3.11 us (2%)
  local copies, waits for them, and re-layouts  1.86 us (1%)
    ppermute x28, waiting for transfers between devices, shift(): return lax.ppermute(v, ax, [(i, (i + s) % n) for i in range(n)])  43.8 us
    ppermute x28, starting transfers between devices, shift(): return lax.ppermute(v, ax, [(i, (i + s) % n) for i in range(n)])  32.9 us
    ppermute x4, waiting for transfers between devices, swap(): lax.ppermute(v, ('xl', 'xh'), [(_x(i), _x(i ^ bit)) for i in range(4)])  13.8 us
    ppermute x6, waiting for transfers between devices, swap(): return lax.ppermute(v, ax, [(i, i ^ bit) for i in range(4)])  13.1 us
    ppermute x4, starting transfers between devices, swap(): lax.ppermute(v, ('xl', 'xh'), [(_x(i), _x(i ^ bit)) for i in range(4)])  11.4 us
    ppermute x6, waiting for transfers between devices, shift(): return lax.ppermute(v, ('xl', 'xh'), [(_x(i), _x(i + s)) for i in range(4)])  10.4 us
    ppermute x6, starting transfers between devices, shift(): return lax.ppermute(v, ('xl', 'xh'), [(_x(i), _x(i + s)) for i in range(4)])  10.2 us
    pallas_call x1, Pallas kernels, autoencode(): pl.pallas_call(kernel, in_specs=[SM, VM, VM, VM, VM, VM, HB, VM, VM, VM,...  9.75 us
  transfers between devices with their start and end apart: 44, of which 28 were waited for; matrix products, arithmetic and copies ran while one was open for 1% of the time, Pallas kernels for 5%

profile of v2, /device:TPU:2, one launch (start us, length us, event | category | flops | bytes accessed | tf_op | source)
XLA Modules:
  0.0 173.4 jit_solution(7157039141997716270)
XLA Ops:
  1.0 4.3 %project.3 = (bf16[4,128,512]{2,1,0:T(8,128)(2,1)S(1)}, bf16[2,128,512]{2,1,0:T(8,128)(2,1)S(1)}, bf16[2,128,512]{2,1,0:T(8,128)(2,1)S(1)}, bf16[2,128,512]{2,1,0:T(8,128)(2,1)S(1)}) custom-call(s32[122]{0:T(128)S(1)} %stack.449.table_ref, bf16[128,512]{1,0:T(8,128)(2,1)} %attn_hbm.3, bf16[512,8192]{1,0:T(8,128)(2,1)} %w_ref.5, bf16[16,8192]{1,0:T(8,128)(2,1)} %r_hbm.3), custom_call_target="tpu_custom_call" | custom-call | tf_op jit(solution)/shard_map/project/pallas_call | solution.py:119
  5.4 0.5 collective-permute-start
  5.9 3.1 %collective-permute-start.6 = (bf16[2,128,512]{2,1,0:T(8,128)(2,1)S(1)}, bf16[2,128,512]{2,1,0:T(8,128)(2,1)S(1)}, u32[]{:S(2)}, u32[]{:S(2)}) collective-permute-start(bf16[2,128,512]{2,1,0:T(8,128)(2,1)S(1)} %get-tuple-element.28), channel_id=1, source_target_pairs={{0,96},{32,0},{64,32},{96,64},{1,97},{33,1},{65,33},{97,65},{2,98}... | collective-permute-start | bytes 786440 | tf_op jit(solution)/shard_map/ppermute | solution.py:26
  9.0 2.2 %collective-permute-start.4 = (bf16[2,128,512]{2,1,0:T(8,128)(2,1)S(1)}, bf16[2,128,512]{2,1,0:T(8,128)(2,1)S(1)}, u32[]{:S(2)}, u32[]{:S(2)}) collective-permute-start(bf16[2,128,512]{2,1,0:T(8,128)(2,1)S(1)} %get-tuple-element.26), channel_id=1, source_target_pairs={{0,64},{32,96},{64,0},{96,32},{1,65},{33,97},{65,1},{97,33},{2,66}... | collective-permute-start | bytes 786440 | tf_op jit(solution)/shard_map/ppermute | solution.py:26
  11.2 3.3 %project.2 = (f32[4,128,512]{2,1,0:T(8,128)S(1)}, f32[2,128,512]{2,1,0:T(8,128)S(1)}) custom-call(s32[122]{0:T(128)S(1)} %stack.449.table_ref, bf16[128,512]{1,0:T(8,128)(2,1)} %attn_hbm.3, bf16[512,8192]{1,0:T(8,128)(2,1)} %w_ref.5, bf16[16,8192]{1,0:T(8,128)(2,1)} %r_hbm.3), custom_call_target="tpu_custom_call" | custom-call | tf_op jit(solution)/shard_map/project/pallas_call | solution.py:119
  14.5 5.4 %collective-permute-done.6 = bf16[2,128,512]{2,1,0:T(8,128)(2,1)S(1)} collective-permute-done((bf16[2,128,512]{2,1,0:T(8,128)(2,1)S(1)}, bf16[2,128,512]{2,1,0:T(8,128)(2,1)S(1)}, u32[]{:S(2)}, u32[]{:S(2)}) %collective-permute-start.6) | collective-permute-done | bytes 262176 | tf_op jit(solution)/shard_map/ppermute | solution.py:26
  19.9 3.4 %collective-permute-done.5 = bf16[2,128,512]{2,1,0:T(8,128)(2,1)S(1)} collective-permute-done((bf16[2,128,512]{2,1,0:T(8,128)(2,1)S(1)}, bf16[2,128,512]{2,1,0:T(8,128)(2,1)S(1)}, u32[]{:S(2)}, u32[]{:S(2)}) %collective-permute-start.5) | collective-permute-done | bytes 262176 | tf_op jit(solution)/shard_map/ppermute | solution.py:26
  23.4 1.5 collective-permute-start.7
  25.4 1.7 %collective-permute-start.2 = (bf16[128,512]{1,0:T(8,128)(2,1)S(1)}, bf16[128,512]{1,0:T(8,128)(2,1)S(1)}, u32[]{:S(2)}, u32[]{:S(2)}) collective-permute-start(bf16[128,512]{1,0:T(8,128)(2,1)S(1)} %get-tuple-element.46), channel_id=1, source_target_pairs={{0,32},{32,64},{64,96},{96,0},{1,33},{33,65},{65,97},{97,1},{2,34}... | collective-permute-start | bytes 393224 | tf_op jit(solution)/shard_map/ppermute | solution.py:26
  27.2 0.6 collective-permute-start.1
  27.7 0.7 collective-permute-done.7
  28.5 2.2 %collective-permute-done.3 = bf16[128,512]{1,0:T(8,128)(2,1)S(1)} collective-permute-done((bf16[128,512]{1,0:T(8,128)(2,1)S(1)}, bf16[128,512]{1,0:T(8,128)(2,1)S(1)}, u32[]{:S(2)}, u32[]{:S(2)}) %collective-permute-start.3) | collective-permute-done | bytes 131104 | tf_op jit(solution)/shard_map/ppermute | solution.py:26
  30.8 0.9 collective-permute-done.2
  31.6 2.0 %collective-permute-done.1 = bf16[128,512]{1,0:T(8,128)(2,1)S(1)} collective-permute-done((bf16[128,512]{1,0:T(8,128)(2,1)S(1)}, bf16[128,512]{1,0:T(8,128)(2,1)S(1)}, u32[]{:S(2)}, u32[]{:S(2)}) %collective-permute-start.1) | collective-permute-done | bytes 131104 | tf_op jit(solution)/shard_map/ppermute | solution.py:26
  34.3 1.5 collective-permute-done.12
  36.4 0.5 constant_dynamic-slice_fusion.4
  37.0 2.2 %collective-permute-start.13 = (bf16[128,2,256]{2,0,1:T(8,128)(2,1)S(1)}, bf16[128,2,256]{2,0,1:T(8,128)(2,1)S(1)}, u32[]{:S(2)}, u32[]{:S(2)}) collective-permute-start(bf16[128,2,256]{2,0,1:T(8,128)(2,1)S(1)} %bitcast.298), channel_id=1, source_target_pairs={{0,8},{8,0},{1,9},{9,1},{2,10},{10,2},{3,11},{11,3},{4,12},{12,4},... | collective-permute-start | bytes 393224 | tf_op jit(solution)/shard_map/ppermute | solution.py:26
  39.2 4.9 %collective-permute-done.13 = bf16[128,2,256]{2,0,1:T(8,128)(2,1)S(1)} collective-permute-done((bf16[128,2,256]{2,0,1:T(8,128)(2,1)S(1)}, bf16[128,2,256]{2,0,1:T(8,128)(2,1)S(1)}, u32[]{:S(2)}, u32[]{:S(2)}) %collective-permute-start.13) | collective-permute-done | bytes 131104 | tf_op jit(solution)/shard_map/ppermute | solution.py:26
  44.2 2.0 %collective-permute-start.14 = (bf16[128,2,256]{2,0,1:T(8,128)(2,1)S(1)}, bf16[128,2,256]{2,0,1:T(8,128)(2,1)S(1)}, u32[]{:S(2)}, u32[]{:S(2)}) collective-permute-start(bf16[128,2,256]{2,0,1:T(8,128)(2,1)S(1)} %fusion.24), channel_id=1, source_target_pairs={{0,2},{2,0},{4,6},{6,4},{1,3},{3,1},{5,7},{7,5},{8,10},{10,8},{12,... | collective-permute-start | bytes 393224 | tf_op jit(solution)/shard_map/ppermute | solution.py:62
  46.2 3.1 %collective-permute-done.14 = bf16[128,2,256]{2,0,1:T(8,128)(2,1)S(1)} collective-permute-done((bf16[128,2,256]{2,0,1:T(8,128)(2,1)S(1)}, bf16[128,2,256]{2,0,1:T(8,128)(2,1)S(1)}, u32[]{:S(2)}, u32[]{:S(2)}) %collective-permute-start.14) | collective-permute-done | bytes 131104 | tf_op jit(solution)/shard_map/ppermute | solution.py:62
  49.3 4.0 %collective-permute-start.15 = (bf16[128,2,256]{2,0,1:T(8,128)(2,1)S(1)}, bf16[128,2,256]{2,0,1:T(8,128)(2,1)S(1)}, u32[]{:S(2)}, u32[]{:S(2)}) collective-permute-start(bf16[128,2,256]{2,0,1:T(8,128)(2,1)S(1)} %add.702), channel_id=1, source_target_pairs={{0,4},{2,6},{4,0},{6,2},{1,5},{3,7},{5,1},{7,3},{8,12},{10,14},{12... | collective-permute-start | bytes 393224 | tf_op jit(solution)/shard_map/ppermute | solution.py:62
  53.2 2.9 %collective-permute-done.15 = bf16[128,2,256]{2,0,1:T(8,128)(2,1)S(1)} collective-permute-done((bf16[128,2,256]{2,0,1:T(8,128)(2,1)S(1)}, bf16[128,2,256]{2,0,1:T(8,128)(2,1)S(1)}, u32[]{:S(2)}, u32[]{:S(2)}) %collective-permute-start.15) | collective-permute-done | bytes 131104 | tf_op jit(solution)/shard_map/ppermute | solution.py:62
  56.3 0.6 collective-permute-start.16
  56.8 3.8 %collective-permute-done.16 = bf16[128,256]{1,0:T(8,128)(2,1)S(1)} collective-permute-done((bf16[128,256]{1,0:T(8,128)(2,1)S(1)}, bf16[128,256]{1,0:T(8,128)(2,1)S(1)}, u32[]{:S(2)}, u32[]{:S(2)}) %collective-permute-start.16) | collective-permute-done | bytes 65568 | tf_op jit(solution)/shard_map/ppermute | solution.py:61
  60.6 2.9 %collective-permute-start.17 = (bf16[2,128,256]{2,1,0:T(8,128)(2,1)S(1)}, bf16[2,128,256]{2,1,0:T(8,128)(2,1)S(1)}, u32[]{:S(2)}, u32[]{:S(2)}) collective-permute-start(bf16[2,128,256]{2,1,0:T(8,128)(2,1)S(1)} %pad_maximum_fusion.9), channel_id=1, source_target_pairs={{0,8},{16,24},{8,0},{24,16},{1,9},{17,25},{9,1},{25,17},{2,10},{18... | collective-permute-start | bytes 393224 | tf_op jit(solution)/shard_map/ppermute | solution.py:61
  63.5 3.7 %collective-permute-done.17 = bf16[2,128,256]{2,1,0:T(8,128)(2,1)S(1)} collective-permute-done((bf16[2,128,256]{2,1,0:T(8,128)(2,1)S(1)}, bf16[2,128,256]{2,1,0:T(8,128)(2,1)S(1)}, u32[]{:S(2)}, u32[]{:S(2)}) %collective-permute-start.17) | collective-permute-done | bytes 131104 | tf_op jit(solution)/shard_map/ppermute | solution.py:61
  67.2 1.6 collective-permute-start.23
  68.8 1.1 collective-permute-start.19
  69.9 2.5 %collective-permute-start.22 = (bf16[4,128,256]{2,1,0:T(8,128)(2,1)S(1)}, bf16[4,128,256]{2,1,0:T(8,128)(2,1)S(1)}, u32[]{:S(2)}, u32[]{:S(2)}) collective-permute-start(bf16[4,128,256]{2,1,0:T(8,128)(2,1)S(1)} %get-tuple-element.61), channel_id=1, source_target_pairs={{0,64},{32,96},{64,0},{96,32},{1,65},{33,97},{65,1},{97,33},{2,66}... | collective-permute-start | bytes 786440 | tf_op jit(solution)/shard_map/ppermute | solution.py:26
  72.4 0.5 collective-permute-start.21
  72.9 3.8 %collective-permute-done.19 = bf16[2,128,256]{2,1,0:T(8,128)(2,1)S(1)} collective-permute-done((bf16[2,128,256]{2,1,0:T(8,128)(2,1)S(1)}, bf16[2,128,256]{2,1,0:T(8,128)(2,1)S(1)}, u32[]{:S(2)}, u32[]{:S(2)}) %collective-permute-start.19) | collective-permute-done | bytes 131104 | tf_op jit(solution)/shard_map/ppermute | solution.py:62
  76.8 0.6 collective-permute-start.27
  77.4 2.2 %collective-permute-start.26 = (bf16[4,128,256]{2,1,0:T(8,128)(2,1)S(1)}, bf16[4,128,256]{2,1,0:T(8,128)(2,1)S(1)}, u32[]{:S(2)}, u32[]{:S(2)}) collective-permute-start(bf16[4,128,256]{2,1,0:T(8,128)(2,1)S(1)} %get-tuple-element.59), channel_id=1, source_target_pairs={{0,8},{16,24},{8,0},{24,16},{1,9},{17,25},{9,1},{25,17},{2,10},{18... | collective-permute-start | bytes 786440 | tf_op jit(solution)/shard_map/ppermute | solution.py:24
  79.6 1.8 %collective-permute-start.25 = (bf16[4,128,256]{2,1,0:T(8,128)(2,1)S(1)}, bf16[4,128,256]{2,1,0:T(8,128)(2,1)S(1)}, u32[]{:S(2)}, u32[]{:S(2)}) collective-permute-start(bf16[4,128,256]{2,1,0:T(8,128)(2,1)S(1)} %get-tuple-element.59), channel_id=1, source_target_pairs={{0,16},{16,8},{8,24},{24,0},{1,17},{17,9},{9,25},{25,1},{2,18},{18... | collective-permute-start | bytes 786440 | tf_op jit(solution)/shard_map/ppermute | solution.py:24
  81.4 1.3 collective-permute-done.21
  83.2 3.5 %collective-permute-done.26 = bf16[4,128,256]{2,1,0:T(8,128)(2,1)S(1)} collective-permute-done((bf16[4,128,256]{2,1,0:T(8,128)(2,1)S(1)}, bf16[4,128,256]{2,1,0:T(8,128)(2,1)S(1)}, u32[]{:S(2)}, u32[]{:S(2)}) %collective-permute-start.26) | collective-permute-done | bytes 262176 | tf_op jit(solution)/shard_map/ppermute | solution.py:24
  86.8 1.4 collective-permute-done.25
  88.4 0.8 collective-permute-start.20
  89.2 2.2 %collective-permute-done.20.oth_ref = bf16[2,4,128,256]{3,2,1,0:T(8,128)(2,1)S(1)} collective-permute-done((bf16[2,4,128,256]{3,2,1,0:T(8,128)(2,1)S(1)}, bf16[2,4,128,256]{3,2,1,0:T(8,128)(2,1)S(1)}, u32[]{:S(2)}, u32[]{:S(2)}) %collective-permute-start.20) | collective-permute-done | bytes 524320 | tf_op jit(solution)/shard_map/ppermute | solution.py:26
  91.4 3.6 %first_terms.1.acc_ref = f32[256,1024]{1,0:T(8,128)S(1)} custom-call(s32[122]{0:T(128)S(1)} %stack.449.table_ref, bf16[2,4,128,256]{3,2,1,0:T(8,128)(2,1)S(1)} %pad_maximum_fusion.2.own_ref, bf16[2,4,128,256]{3,2,1,0:T(8,128)(2,1)S(1)} %collective-permute-done.20.oth_ref, bf16[8192,1024]{1,0:T(8,128)(2,1)} %w_ref.7, f32[32,1,256]{2,1,0:T(1,128)S(1)} %bitcast.272), custom_call_target="tpu_custom_call" | custom-call | tf_op jit(solution)/shard_map/first_terms/pallas_call | solution.py:162
  95.0 9.7 %autoencode.1 = (bf16[256,1024]{1,0:T(8,128)(2,1)S(1)}, bf16[256,1024]{1,0:T(8,128)(2,1)}, f32[128,4096]{1,0:T(8,128)S(1)}, bf16[128,4096]{1,0:T(8,128)(2,1)S(1)}, bf16[4096,1024]{1,0:T(8,128)(2,1)S(1)}) custom-call(s32[122]{0:T(128)S(1)} %stack.449.table_ref, f32[256,1024]{1,0:T(8,128)S(1)} %first_terms.1.acc_ref, ...), custom_call_target="tpu_custom_call" | custom-call | tf_op jit(solution)/shard_map/autoencode/pallas_call | solution.py:221
  105.0 2.6 %collective-permute-start.8 = (bf16[4,16,1024]{2,1,0:T(8,128)(2,1)S(1)}, bf16[4,16,1024]{2,1,0:T(8,128)(2,1)S(1)}, u32[]{:S(2)}, u32[]{:S(2)}) collective-permute-start(bf16[4,16,1024]{2,1,0:T(8,128)(2,1)S(1)} %get-tuple-element.65), channel_id=1, source_target_pairs={{0,16},{16,0},{1,17},{17,1},{2,18},{18,2},{3,19},{19,3},{4,20},{20... | collective-permute-start | bytes 393224 | tf_op jit(solution)/shard_map/ppermute | solution.py:26
  107.6 4.0 %collective-permute-done.8 = bf16[4,16,1024]{2,1,0:T(8,128)(2,1)S(1)} collective-permute-done((bf16[4,16,1024]{2,1,0:T(8,128)(2,1)S(1)}, bf16[4,16,1024]{2,1,0:T(8,128)(2,1)S(1)}, u32[]{:S(2)}, u32[]{:S(2)}) %collective-permute-start.8) | collective-permute-done | bytes 131104 | tf_op jit(solution)/shard_map/ppermute | solution.py:26
  111.6 1.6 collective-permute-start.9
  113.2 3.4 %collective-permute-start.10 = (bf16[2,16,1024]{2,1,0:T(8,128)(2,1)S(1)}, bf16[2,16,1024]{2,1,0:T(8,128)(2,1)S(1)}, u32[]{:S(2)}, u32[]{:S(2)}) collective-permute-start(bf16[2,16,1024]{2,1,0:T(8,128)(2,1)S(1)} %get-tuple-element.57), channel_id=1, source_target_pairs={{0,64},{32,96},{64,0},{96,32},{1,65},{33,97},{65,1},{97,33},{2,66}... | collective-permute-start | bytes 196616 | tf_op jit(solution)/shard_map/ppermute | solution.py:26
  116.5 2.4 %decode.1 = (f32[128,4096]{1,0:T(8,128)S(1)}, bf16[128,4096]{1,0:T(8,128)(2,1)S(1)}) custom-call(bf16[256,1024]{1,0:T(8,128)(2,1)S(1)} %get-tuple-element.31.codes_ref, bf16[4096,1024]{1,0:T(8,128)(2,1)S(1)} %get-tuple-element.32.w_ref), custom_call_target="tpu_custom_call" | custom-call | tf_op jit(solution)/shard_map/decode/pallas_call | solution.py:244
  119.7 2.0 %collective-permute-start.31 = (bf16[4,8,4096]{2,1,0:T(8,128)(2,1)S(1)}, bf16[4,8,4096]{2,1,0:T(8,128)(2,1)S(1)}, u32[]{:S(2)}, u32[]{:S(2)}) collective-permute-start(bf16[4,8,4096]{2,1,0:T(8,128)(2,1)S(1)} %get-tuple-element.52), channel_id=1, source_target_pairs={{0,32},{32,64},{64,96},{96,0},{1,33},{33,65},{65,97},{97,1},{2,34}... | collective-permute-start | bytes 786440 | tf_op jit(solution)/shard_map/ppermute | solution.py:26
  122.2 6.7 %collective-permute-done.32 = bf16[4,8,4096]{2,1,0:T(8,128)(2,1)S(1)} collective-permute-done((bf16[4,8,4096]{2,1,0:T(8,128)(2,1)S(1)}, bf16[4,8,4096]{2,1,0:T(8,128)(2,1)S(1)}, u32[]{:S(2)}, u32[]{:S(2)}) %collective-permute-start.32) | collective-permute-done | bytes 262176 | tf_op jit(solution)/shard_map/ppermute | solution.py:26
  128.9 1.7 %collective-permute-start.38 = (bf16[4,8,4096]{2,1,0:T(8,128)(2,1)S(1)}, bf16[4,8,4096]{2,1,0:T(8,128)(2,1)S(1)}, u32[]{:S(2)}, u32[]{:S(2)}) collective-permute-start(bf16[4,8,4096]{2,1,0:T(8,128)(2,1)S(1)} %get-tuple-element.48), channel_id=1, source_target_pairs={{0,24},{16,0},{8,16},{24,8},{1,25},{17,1},{9,17},{25,9},{2,26},{18... | collective-permute-start | bytes 786440 | tf_op jit(solution)/shard_map/ppermute | solution.py:24
  130.6 4.7 %collective-permute-done.31 = bf16[4,8,4096]{2,1,0:T(8,128)(2,1)S(1)} collective-permute-done((bf16[4,8,4096]{2,1,0:T(8,128)(2,1)S(1)}, bf16[4,8,4096]{2,1,0:T(8,128)(2,1)S(1)}, u32[]{:S(2)}, u32[]{:S(2)}) %collective-permute-start.31) | collective-permute-done | bytes 262176 | tf_op jit(solution)/shard_map/ppermute | solution.py:26
  135.3 0.6 collective-permute-start.37
  135.9 3.2 %collective-permute-start.36 = (bf16[4,8,4096]{2,1,0:T(8,128)(2,1)S(1)}, bf16[4,8,4096]{2,1,0:T(8,128)(2,1)S(1)}, u32[]{:S(2)}, u32[]{:S(2)}) collective-permute-start(bf16[4,8,4096]{2,1,0:T(8,128)(2,1)S(1)} %get-tuple-element.47), channel_id=1, source_target_pairs={{0,8},{16,24},{8,0},{24,16},{1,9},{17,25},{9,1},{25,17},{2,10},{18... | collective-permute-start | bytes 786440 | tf_op jit(solution)/shard_map/ppermute | solution.py:24
  139.4 5.1 %collective-permute-done.37 = bf16[4,8,4096]{2,1,0:T(8,128)(2,1)S(1)} collective-permute-done((bf16[4,8,4096]{2,1,0:T(8,128)(2,1)S(1)}, bf16[4,8,4096]{2,1,0:T(8,128)(2,1)S(1)}, u32[]{:S(2)}, u32[]{:S(2)}) %collective-permute-start.37) | collective-permute-done | bytes 262176 | tf_op jit(solution)/shard_map/ppermute | solution.py:24
  144.5 7.0 %collective-permute-start.33 = (bf16[2,8,4096]{2,1,0:T(8,128)(2,1)S(1)}, bf16[2,8,4096]{2,1,0:T(8,128)(2,1)S(1)}, u32[]{:S(2)}, u32[]{:S(2)}) collective-permute-start(bf16[2,8,4096]{2,1,0:T(8,128)(2,1)S(1)} %fusion.18), channel_id=1, source_target_pairs={{0,16},{16,0},{8,24},{24,8},{1,17},{17,1},{9,25},{25,9},{2,18},{18... | collective-permute-start | bytes 393224 | tf_op jit(solution)/shard_map/ppermute | solution.py:61
  151.8 2.8 %collective-permute-done.33 = bf16[2,8,4096]{2,1,0:T(8,128)(2,1)S(1)} collective-permute-done((bf16[2,8,4096]{2,1,0:T(8,128)(2,1)S(1)}, bf16[2,8,4096]{2,1,0:T(8,128)(2,1)S(1)}, u32[]{:S(2)}, u32[]{:S(2)}) %collective-permute-start.33) | collective-permute-done | bytes 131104 | tf_op jit(solution)/shard_map/ppermute | solution.py:61
  154.6 1.0 collective-permute-start.34
  155.5 1.2 collective-permute-done.39
  156.9 3.6 %collective-permute-done.34 = bf16[8,4096]{1,0:T(8,128)(2,1)S(1)} collective-permute-done((bf16[8,4096]{1,0:T(8,128)(2,1)S(1)}, bf16[8,4096]{1,0:T(8,128)(2,1)S(1)}, u32[]{:S(2)}, u32[]{:S(2)}) %collective-permute-start.34) | collective-permute-done | bytes 65568 | tf_op jit(solution)/shard_map/ppermute | solution.py:61
  160.6 2.1 %collective-permute-done.40 = bf16[8,4096]{1,0:T(8,128)(2,1)S(1)} collective-permute-done((bf16[8,4096]{1,0:T(8,128)(2,1)S(1)}, bf16[8,4096]{1,0:T(8,128)(2,1)S(1)}, u32[]{:S(2)}, u32[]{:S(2)}) %collective-permute-start.40) | collective-permute-done | bytes 65568 | tf_op jit(solution)/shard_map/ppermute | solution.py:62
  163.2 3.4 %collective-permute-start.43 = (bf16[2,8192]{1,0:T(2,128)(2,1)S(1)}, bf16[2,8192]{1,0:T(2,128)(2,1)S(1)}, u32[]{:S(2)}, u32[]{:S(2)}) collective-permute-start(bf16[2,8192]{1,0:T(2,128)(2,1)S(1)} %get-tuple-element.68), channel_id=1, source_target_pairs={{0,6},{2,0},{4,2},{6,4},{1,7},{3,1},{5,3},{7,5},{8,14},{10,8},{12,... | collective-permute-start | bytes 98312 | tf_op jit(solution)/shard_map/ppermute | solution.py:26
  166.6 1.5 collective-permute-start.41
  168.2 3.5 %collective-permute-done.42 = bf16[2,8192]{1,0:T(2,128)(2,1)S(1)} collective-permute-done((bf16[2,8192]{1,0:T(2,128)(2,1)S(1)}, bf16[2,8192]{1,0:T(2,128)(2,1)S(1)}, u32[]{:S(2)}, u32[]{:S(2)}) %collective-permute-start.42) | collective-permute-done | bytes 32800 | tf_op jit(solution)/shard_map/ppermute | solution.py:26
  172.1 0.8 multiply_reduce_fusion
  172.9 0.5 broadcast_multiply_fusion
  (112 shorter events, 6.3 us)
Async XLA Ops:
  5.4 19.6 %collective-permute-start = (bf16[4,128,512]{2,1,0:T(8,128)(2,1)S(1)}, bf16[4,128,512]{2,1,0:T(8,128)(2,1)S(1)}, u32[]{:S(2)}, u32[]{:S(2)}) collective-permute-start(bf16[4,128,512]{2,1,0:T(8,128)(2,1)S(1)} %get-tuple-element.24), channel_id=1, source_target_pairs={{0,16},{16,0},{1,17},{17,1},{2,18},{18,2},{3,19},{19,3},{4,20},{20... | collective-permute-start | bytes 1572872 | tf_op jit(solution)/shard_map/ppermute | solution.py:26
  5.9 14.1 %collective-permute-start.6 = (bf16[2,128,512]{2,1,0:T(8,128)(2,1)S(1)}, bf16[2,128,512]{2,1,0:T(8,128)(2,1)S(1)}, u32[]{:S(2)}, u32[]{:S(2)}) collective-permute-start(bf16[2,128,512]{2,1,0:T(8,128)(2,1)S(1)} %get-tuple-element.28), channel_id=1, source_target_pairs={{0,96},{32,0},{64,32},{96,64},{1,97},{33,1},{65,33},{97,65},{2,98}... | collective-permute-start | bytes 786440 | tf_op jit(solution)/shard_map/ppermute | solution.py:26
  9.0 14.3 %collective-permute-start.5 = (bf16[2,128,512]{2,1,0:T(8,128)(2,1)S(1)}, bf16[2,128,512]{2,1,0:T(8,128)(2,1)S(1)}, u32[]{:S(2)}, u32[]{:S(2)}) collective-permute-start(bf16[2,128,512]{2,1,0:T(8,128)(2,1)S(1)} %get-tuple-element.27), channel_id=1, source_target_pairs={{0,32},{32,64},{64,96},{96,0},{1,33},{33,65},{65,97},{97,1},{2,34}... | collective-permute-start | bytes 786440 | tf_op jit(solution)/shard_map/ppermute | solution.py:26
  9.0 14.3 %collective-permute-start.4 = (bf16[2,128,512]{2,1,0:T(8,128)(2,1)S(1)}, bf16[2,128,512]{2,1,0:T(8,128)(2,1)S(1)}, u32[]{:S(2)}, u32[]{:S(2)}) collective-permute-start(bf16[2,128,512]{2,1,0:T(8,128)(2,1)S(1)} %get-tuple-element.26), channel_id=1, source_target_pairs={{0,64},{32,96},{64,0},{96,32},{1,65},{33,97},{65,1},{97,33},{2,66}... | collective-permute-start | bytes 786440 | tf_op jit(solution)/shard_map/ppermute | solution.py:26
  23.3 10.4 %copy-start.4 = (s32[256]{0:T(256)S(1)}, s32[256]{0:T(256)}, u32[]{:S(2)}) copy-start(s32[256]{0:T(256)} %param.11) | copy-start | bytes 3076
  23.4 5.0 %collective-permute-start.7 = (bf16[128,512]{1,0:T(8,128)(2,1)S(1)}, bf16[128,512]{1,0:T(8,128)(2,1)S(1)}, u32[]{:S(2)}, u32[]{:S(2)}) collective-permute-start(bf16[128,512]{1,0:T(8,128)(2,1)S(1)} %fusion.17), channel_id=1, source_target_pairs={{0,16},{16,0},{1,17},{17,1},{2,18},{18,2},{3,19},{19,3},{4,20},{20... | collective-permute-start | bytes 393224 | tf_op jit(solution)/shard_map/ppermute | solution.py:26
  25.1 5.7 %collective-permute-start.3 = (bf16[128,512]{1,0:T(8,128)(2,1)S(1)}, bf16[128,512]{1,0:T(8,128)(2,1)S(1)}, u32[]{:S(2)}, u32[]{:S(2)}) collective-permute-start(bf16[128,512]{1,0:T(8,128)(2,1)S(1)} %get-tuple-element.45), channel_id=1, source_target_pairs={{0,96},{32,0},{64,32},{96,64},{1,97},{33,1},{65,33},{97,65},{2,98}... | collective-permute-start | bytes 393224 | tf_op jit(solution)/shard_map/ppermute | solution.py:26
  25.4 6.2 %collective-permute-start.2 = (bf16[128,512]{1,0:T(8,128)(2,1)S(1)}, bf16[128,512]{1,0:T(8,128)(2,1)S(1)}, u32[]{:S(2)}, u32[]{:S(2)}) collective-permute-start(bf16[128,512]{1,0:T(8,128)(2,1)S(1)} %get-tuple-element.46), channel_id=1, source_target_pairs={{0,32},{32,64},{64,96},{96,0},{1,33},{33,65},{65,97},{97,1},{2,34}... | collective-permute-start | bytes 393224 | tf_op jit(solution)/shard_map/ppermute | solution.py:26
  27.2 6.5 %collective-permute-start.1 = (bf16[128,512]{1,0:T(8,128)(2,1)S(1)}, bf16[128,512]{1,0:T(8,128)(2,1)S(1)}, u32[]{:S(2)}, u32[]{:S(2)}) collective-permute-start(bf16[128,512]{1,0:T(8,128)(2,1)S(1)} %get-tuple-element.44), channel_id=1, source_target_pairs={{0,64},{32,96},{64,0},{96,32},{1,65},{33,97},{65,1},{97,33},{2,66}... | collective-permute-start | bytes 393224 | tf_op jit(solution)/shard_map/ppermute | solution.py:26
  34.2 1.6 collective-permute-start.12
  37.0 7.1 %collective-permute-start.13 = (bf16[128,2,256]{2,0,1:T(8,128)(2,1)S(1)}, bf16[128,2,256]{2,0,1:T(8,128)(2,1)S(1)}, u32[]{:S(2)}, u32[]{:S(2)}) collective-permute-start(bf16[128,2,256]{2,0,1:T(8,128)(2,1)S(1)} %bitcast.298), channel_id=1, source_target_pairs={{0,8},{8,0},{1,9},{9,1},{2,10},{10,2},{3,11},{11,3},{4,12},{12,4},... | collective-permute-start | bytes 393224 | tf_op jit(solution)/shard_map/ppermute | solution.py:26
  44.2 5.0 %collective-permute-start.14 = (bf16[128,2,256]{2,0,1:T(8,128)(2,1)S(1)}, bf16[128,2,256]{2,0,1:T(8,128)(2,1)S(1)}, u32[]{:S(2)}, u32[]{:S(2)}) collective-permute-start(bf16[128,2,256]{2,0,1:T(8,128)(2,1)S(1)} %fusion.24), channel_id=1, source_target_pairs={{0,2},{2,0},{4,6},{6,4},{1,3},{3,1},{5,7},{7,5},{8,10},{10,8},{12,... | collective-permute-start | bytes 393224 | tf_op jit(solution)/shard_map/ppermute | solution.py:62
  49.3 6.9 %collective-permute-start.15 = (bf16[128,2,256]{2,0,1:T(8,128)(2,1)S(1)}, bf16[128,2,256]{2,0,1:T(8,128)(2,1)S(1)}, u32[]{:S(2)}, u32[]{:S(2)}) collective-permute-start(bf16[128,2,256]{2,0,1:T(8,128)(2,1)S(1)} %add.702), channel_id=1, source_target_pairs={{0,4},{2,6},{4,0},{6,2},{1,5},{3,7},{5,1},{7,3},{8,12},{10,14},{12... | collective-permute-start | bytes 393224 | tf_op jit(solution)/shard_map/ppermute | solution.py:62
  56.3 4.3 %collective-permute-start.16 = (bf16[128,256]{1,0:T(8,128)(2,1)S(1)}, bf16[128,256]{1,0:T(8,128)(2,1)S(1)}, u32[]{:S(2)}, u32[]{:S(2)}) collective-permute-start(bf16[128,256]{1,0:T(8,128)(2,1)S(1)} %get-tuple-element.71), channel_id=1, source_target_pairs={{0,16},{16,0},{8,24},{24,8},{1,17},{17,1},{9,25},{25,9},{2,18},{18... | collective-permute-start | bytes 196616 | tf_op jit(solution)/shard_map/ppermute | solution.py:61
  60.6 6.6 %collective-permute-start.17 = (bf16[2,128,256]{2,1,0:T(8,128)(2,1)S(1)}, bf16[2,128,256]{2,1,0:T(8,128)(2,1)S(1)}, u32[]{:S(2)}, u32[]{:S(2)}) collective-permute-start(bf16[2,128,256]{2,1,0:T(8,128)(2,1)S(1)} %pad_maximum_fusion.9), channel_id=1, source_target_pairs={{0,8},{16,24},{8,0},{24,16},{1,9},{17,25},{9,1},{25,17},{2,10},{18... | collective-permute-start | bytes 393224 | tf_op jit(solution)/shard_map/ppermute | solution.py:61
  63.5 5.3 %collective-permute-start.18 = (bf16[128,256]{1,0:T(8,128)(2,1)S(1)}, bf16[128,256]{1,0:T(8,128)(2,1)S(1)}, u32[]{:S(2)}, u32[]{:S(2)}) collective-permute-start(bf16[128,256]{1,0:T(8,128)(2,1)S(1)} %get-tuple-element.72), channel_id=1, source_target_pairs={{0,32},{32,0},{64,96},{96,64},{1,33},{33,1},{65,97},{97,65},{2,34}... | collective-permute-start | bytes 196616 | tf_op jit(solution)/shard_map/ppermute | solution.py:62
  67.2 12.4 %collective-permute-start.23 = (bf16[4,128,256]{2,1,0:T(8,128)(2,1)S(1)}, bf16[4,128,256]{2,1,0:T(8,128)(2,1)S(1)}, u32[]{:S(2)}, u32[]{:S(2)}) collective-permute-start(bf16[4,128,256]{2,1,0:T(8,128)(2,1)S(1)} %get-tuple-element.61), channel_id=1, source_target_pairs={{0,96},{32,0},{64,32},{96,64},{1,97},{33,1},{65,33},{97,65},{2,98}... | collective-permute-start | bytes 786440 | tf_op jit(solution)/shard_map/ppermute | solution.py:26
  68.8 8.0 %collective-permute-start.19 = (bf16[2,128,256]{2,1,0:T(8,128)(2,1)S(1)}, bf16[2,128,256]{2,1,0:T(8,128)(2,1)S(1)}, u32[]{:S(2)}, u32[]{:S(2)}) collective-permute-start(bf16[2,128,256]{2,1,0:T(8,128)(2,1)S(1)} %pad_maximum_fusion.10), channel_id=1, source_target_pairs={{0,64},{32,96},{64,0},{96,32},{1,65},{33,97},{65,1},{97,33},{2,66}... | collective-permute-start | bytes 393224 | tf_op jit(solution)/shard_map/ppermute | solution.py:62
  69.9 11.5 %collective-permute-start.22 = (bf16[4,128,256]{2,1,0:T(8,128)(2,1)S(1)}, bf16[4,128,256]{2,1,0:T(8,128)(2,1)S(1)}, u32[]{:S(2)}, u32[]{:S(2)}) collective-permute-start(bf16[4,128,256]{2,1,0:T(8,128)(2,1)S(1)} %get-tuple-element.61), channel_id=1, source_target_pairs={{0,64},{32,96},{64,0},{96,32},{1,65},{33,97},{65,1},{97,33},{2,66}... | collective-permute-start | bytes 786440 | tf_op jit(solution)/shard_map/ppermute | solution.py:26
  72.4 10.3 %collective-permute-start.21 = (bf16[4,128,256]{2,1,0:T(8,128)(2,1)S(1)}, bf16[4,128,256]{2,1,0:T(8,128)(2,1)S(1)}, u32[]{:S(2)}, u32[]{:S(2)}) collective-permute-start(bf16[4,128,256]{2,1,0:T(8,128)(2,1)S(1)} %get-tuple-element.61), channel_id=1, source_target_pairs={{0,32},{32,64},{64,96},{96,0},{1,33},{33,65},{65,97},{97,1},{2,34}... | collective-permute-start | bytes 786440 | tf_op jit(solution)/shard_map/ppermute | solution.py:26
  76.8 6.4 %collective-permute-start.27 = (bf16[4,128,256]{2,1,0:T(8,128)(2,1)S(1)}, bf16[4,128,256]{2,1,0:T(8,128)(2,1)S(1)}, u32[]{:S(2)}, u32[]{:S(2)}) collective-permute-start(bf16[4,128,256]{2,1,0:T(8,128)(2,1)S(1)} %get-tuple-element.59), channel_id=1, source_target_pairs={{0,24},{16,0},{8,16},{24,8},{1,25},{17,1},{9,17},{25,9},{2,26},{18... | collective-permute-start | bytes 786440 | tf_op jit(solution)/shard_map/ppermute | solution.py:24
  77.4 9.4 %collective-permute-start.26 = (bf16[4,128,256]{2,1,0:T(8,128)(2,1)S(1)}, bf16[4,128,256]{2,1,0:T(8,128)(2,1)S(1)}, u32[]{:S(2)}, u32[]{:S(2)}) collective-permute-start(bf16[4,128,256]{2,1,0:T(8,128)(2,1)S(1)} %get-tuple-element.59), channel_id=1, source_target_pairs={{0,8},{16,24},{8,0},{24,16},{1,9},{17,25},{9,1},{25,17},{2,10},{18... | collective-permute-start | bytes 786440 | tf_op jit(solution)/shard_map/ppermute | solution.py:24
  79.6 8.5 %collective-permute-start.25 = (bf16[4,128,256]{2,1,0:T(8,128)(2,1)S(1)}, bf16[4,128,256]{2,1,0:T(8,128)(2,1)S(1)}, u32[]{:S(2)}, u32[]{:S(2)}) collective-permute-start(bf16[4,128,256]{2,1,0:T(8,128)(2,1)S(1)} %get-tuple-element.59), channel_id=1, source_target_pairs={{0,16},{16,8},{8,24},{24,0},{1,17},{17,9},{9,25},{25,1},{2,18},{18... | collective-permute-start | bytes 786440 | tf_op jit(solution)/shard_map/ppermute | solution.py:24
  82.7 8.6 %copy-start = (f32[8192]{0:T(1024)S(1)}, f32[8192]{0:T(1024)}, u32[]{:S(2)}) copy-start(f32[8192]{0:T(1024)} %param.15) | copy-start | bytes 98308
  82.8 12.1 %collective-permute-start.24 = (bf16[3,4,128,256]{3,2,1,0:T(8,128)(2,1)S(1)}, bf16[3,4,128,256]{3,2,1,0:T(8,128)(2,1)S(1)}, u32[]{:S(2)}, u32[]{:S(2)}) collective-permute-start(bf16[3,4,128,256]{3,2,1,0:T(8,128)(2,1)S(1)} %pad_maximum_fusion.oa_ref), channel_id=1, source_target_pairs={{0,1},{1,0},{2,3},{3,2},{4,5},{5,4},{6,7},{7,6},{8,9},{9,8},{10,11... | collective-permute-start | bytes 2359304 | tf_op jit(solution)/shard_map/ppermute | solution.py:26
  88.2 6.7 %collective-permute-start.28 = (bf16[3,4,128,256]{3,2,1,0:T(8,128)(2,1)S(1)}, bf16[3,4,128,256]{3,2,1,0:T(8,128)(2,1)S(1)}, u32[]{:S(2)}, u32[]{:S(2)}) collective-permute-start(bf16[3,4,128,256]{3,2,1,0:T(8,128)(2,1)S(1)} %pad_maximum_fusion.1.ob_ref), channel_id=1, source_target_pairs={{0,1},{1,0},{2,3},{3,2},{4,5},{5,4},{6,7},{7,6},{8,9},{9,8},{10,11... | collective-permute-start | bytes 2359304 | tf_op jit(solution)/shard_map/ppermute | solution.py:26
  88.4 3.0 %collective-permute-start.20 = (bf16[2,4,128,256]{3,2,1,0:T(8,128)(2,1)S(1)}, bf16[2,4,128,256]{3,2,1,0:T(8,128)(2,1)S(1)}, u32[]{:S(2)}, u32[]{:S(2)}) collective-permute-start(bf16[2,4,128,256]{3,2,1,0:T(8,128)(2,1)S(1)} %pad_maximum_fusion.2.own_ref), channel_id=1, source_target_pairs={{0,1},{1,0},{2,3},{3,2},{4,5},{5,4},{6,7},{7,6},{8,9},{9,8},{10,11... | collective-permute-start | bytes 1572872 | tf_op jit(solution)/shard_map/ppermute | solution.py:26
  91.4 3.6 %copy-start.1 = (f32[1024]{0:T(1024)S(1)}, f32[1024]{0:T(1024)}, u32[]{:S(2)}) copy-start(f32[1024]{0:T(1024)} %param.13) | copy-start | bytes 12292
  91.4 3.6 %copy-start.2 = (f32[1024]{0:T(1024)S(1)}, f32[1024]{0:T(1024)}, u32[]{:S(2)}) copy-start(f32[1024]{0:T(1024)} %param.14) | copy-start | bytes 12292
  104.7 14.6 %collective-permute-start.29 = (bf16[128,4096]{1,0:T(8,128)(2,1)S(1)}, bf16[128,4096]{1,0:T(8,128)(2,1)S(1)}, u32[]{:S(2)}, u32[]{:S(2)}) collective-permute-start(bf16[128,4096]{1,0:T(8,128)(2,1)S(1)} %get-tuple-element.30), channel_id=1, source_target_pairs={{0,1},{1,0},{2,3},{3,2},{4,5},{5,4},{6,7},{7,6},{8,9},{9,8},{10,11... | collective-permute-start | bytes 3145736 | tf_op jit(solution)/shard_map/ppermute | solution.py:26
  105.0 6.6 %collective-permute-start.8 = (bf16[4,16,1024]{2,1,0:T(8,128)(2,1)S(1)}, bf16[4,16,1024]{2,1,0:T(8,128)(2,1)S(1)}, u32[]{:S(2)}, u32[]{:S(2)}) collective-permute-start(bf16[4,16,1024]{2,1,0:T(8,128)(2,1)S(1)} %get-tuple-element.65), channel_id=1, source_target_pairs={{0,16},{16,0},{1,17},{17,1},{2,18},{18,2},{3,19},{19,3},{4,20},{20... | collective-permute-start | bytes 393224 | tf_op jit(solution)/shard_map/ppermute | solution.py:26
  111.6 51.2 %collective-permute-start.9 = (bf16[2,16,1024]{2,1,0:T(8,128)(2,1)S(1)}, bf16[2,16,1024]{2,1,0:T(8,128)(2,1)S(1)}, u32[]{:S(2)}, u32[]{:S(2)}) collective-permute-start(bf16[2,16,1024]{2,1,0:T(8,128)(2,1)S(1)} %get-tuple-element.56), channel_id=1, source_target_pairs={{0,32},{32,64},{64,96},{96,0},{1,33},{33,65},{65,97},{97,1},{2,34}... | collective-permute-start | bytes 196616 | tf_op jit(solution)/shard_map/ppermute | solution.py:26
  113.2 49.7 %collective-permute-start.10 = (bf16[2,16,1024]{2,1,0:T(8,128)(2,1)S(1)}, bf16[2,16,1024]{2,1,0:T(8,128)(2,1)S(1)}, u32[]{:S(2)}, u32[]{:S(2)}) collective-permute-start(bf16[2,16,1024]{2,1,0:T(8,128)(2,1)S(1)} %get-tuple-element.57), channel_id=1, source_target_pairs={{0,64},{32,96},{64,0},{96,32},{1,65},{33,97},{65,1},{97,33},{2,66}... | collective-permute-start | bytes 196616 | tf_op jit(solution)/shard_map/ppermute | solution.py:26
  118.9 2.8 %collective-permute-start.35 = (bf16[128,4096]{1,0:T(8,128)(2,1)S(1)}, bf16[128,4096]{1,0:T(8,128)(2,1)S(1)}, u32[]{:S(2)}, u32[]{:S(2)}) collective-permute-start(bf16[128,4096]{1,0:T(8,128)(2,1)S(1)} %get-tuple-element.34), channel_id=1, source_target_pairs={{0,1},{1,0},{2,3},{3,2},{4,5},{5,4},{6,7},{7,6},{8,9},{9,8},{10,11... | collective-permute-start | bytes 3145736 | tf_op jit(solution)/shard_map/ppermute | solution.py:26
  119.6 9.2 %collective-permute-start.32 = (bf16[4,8,4096]{2,1,0:T(8,128)(2,1)S(1)}, bf16[4,8,4096]{2,1,0:T(8,128)(2,1)S(1)}, u32[]{:S(2)}, u32[]{:S(2)}) collective-permute-start(bf16[4,8,4096]{2,1,0:T(8,128)(2,1)S(1)} %get-tuple-element.51), channel_id=1, source_target_pairs={{0,96},{32,0},{64,32},{96,64},{1,97},{33,1},{65,33},{97,65},{2,98}... | collective-permute-start | bytes 786440 | tf_op jit(solution)/shard_map/ppermute | solution.py:26
  119.7 15.6 %collective-permute-start.31 = (bf16[4,8,4096]{2,1,0:T(8,128)(2,1)S(1)}, bf16[4,8,4096]{2,1,0:T(8,128)(2,1)S(1)}, u32[]{:S(2)}, u32[]{:S(2)}) collective-permute-start(bf16[4,8,4096]{2,1,0:T(8,128)(2,1)S(1)} %get-tuple-element.52), channel_id=1, source_target_pairs={{0,32},{32,64},{64,96},{96,0},{1,33},{33,65},{65,97},{97,1},{2,34}... | collective-permute-start | bytes 786440 | tf_op jit(solution)/shard_map/ppermute | solution.py:26
  121.7 14.2 %collective-permute-start.30 = (bf16[4,8,4096]{2,1,0:T(8,128)(2,1)S(1)}, bf16[4,8,4096]{2,1,0:T(8,128)(2,1)S(1)}, u32[]{:S(2)}, u32[]{:S(2)}) collective-permute-start(bf16[4,8,4096]{2,1,0:T(8,128)(2,1)S(1)} %get-tuple-element.50), channel_id=1, source_target_pairs={{0,64},{32,96},{64,0},{96,32},{1,65},{33,97},{65,1},{97,33},{2,66}... | collective-permute-start | bytes 786440 | tf_op jit(solution)/shard_map/ppermute | solution.py:26
  128.9 10.4 %collective-permute-start.38 = (bf16[4,8,4096]{2,1,0:T(8,128)(2,1)S(1)}, bf16[4,8,4096]{2,1,0:T(8,128)(2,1)S(1)}, u32[]{:S(2)}, u32[]{:S(2)}) collective-permute-start(bf16[4,8,4096]{2,1,0:T(8,128)(2,1)S(1)} %get-tuple-element.48), channel_id=1, source_target_pairs={{0,24},{16,0},{8,16},{24,8},{1,25},{17,1},{9,17},{25,9},{2,26},{18... | collective-permute-start | bytes 786440 | tf_op jit(solution)/shard_map/ppermute | solution.py:24
  135.3 9.2 %collective-permute-start.37 = (bf16[4,8,4096]{2,1,0:T(8,128)(2,1)S(1)}, bf16[4,8,4096]{2,1,0:T(8,128)(2,1)S(1)}, u32[]{:S(2)}, u32[]{:S(2)}) collective-permute-start(bf16[4,8,4096]{2,1,0:T(8,128)(2,1)S(1)} %get-tuple-element.49), channel_id=1, source_target_pairs={{0,16},{16,8},{8,24},{24,0},{1,17},{17,9},{9,25},{25,1},{2,18},{18... | collective-permute-start | bytes 786440 | tf_op jit(solution)/shard_map/ppermute | solution.py:24
  135.9 15.6 %collective-permute-start.36 = (bf16[4,8,4096]{2,1,0:T(8,128)(2,1)S(1)}, bf16[4,8,4096]{2,1,0:T(8,128)(2,1)S(1)}, u32[]{:S(2)}, u32[]{:S(2)}) collective-permute-start(bf16[4,8,4096]{2,1,0:T(8,128)(2,1)S(1)} %get-tuple-element.47), channel_id=1, source_target_pairs={{0,8},{16,24},{8,0},{24,16},{1,9},{17,25},{9,1},{25,17},{2,10},{18... | collective-permute-start | bytes 786440 | tf_op jit(solution)/shard_map/ppermute | solution.py:24
  139.3 23.6 %collective-permute-start.11 = (bf16[2,16,1024]{2,1,0:T(8,128)(2,1)S(1)}, bf16[2,16,1024]{2,1,0:T(8,128)(2,1)S(1)}, u32[]{:S(2)}, u32[]{:S(2)}) collective-permute-start(bf16[2,16,1024]{2,1,0:T(8,128)(2,1)S(1)} %get-tuple-element.58), channel_id=1, source_target_pairs={{0,96},{32,0},{64,32},{96,64},{1,97},{33,1},{65,33},{97,65},{2,98}... | collective-permute-start | bytes 196616 | tf_op jit(solution)/shard_map/ppermute | solution.py:26
  144.5 10.0 %collective-permute-start.33 = (bf16[2,8,4096]{2,1,0:T(8,128)(2,1)S(1)}, bf16[2,8,4096]{2,1,0:T(8,128)(2,1)S(1)}, u32[]{:S(2)}, u32[]{:S(2)}) collective-permute-start(bf16[2,8,4096]{2,1,0:T(8,128)(2,1)S(1)} %fusion.18), channel_id=1, source_target_pairs={{0,16},{16,0},{8,24},{24,8},{1,17},{17,1},{9,25},{25,9},{2,18},{18... | collective-permute-start | bytes 393224 | tf_op jit(solution)/shard_map/ppermute | solution.py:61
  151.7 5.0 %collective-permute-start.39 = (bf16[2,8,4096]{2,1,0:T(8,128)(2,1)S(1)}, bf16[2,8,4096]{2,1,0:T(8,128)(2,1)S(1)}, u32[]{:S(2)}, u32[]{:S(2)}) collective-permute-start(bf16[2,8,4096]{2,1,0:T(8,128)(2,1)S(1)} %fusion.19), channel_id=1, source_target_pairs={{0,32},{32,0},{64,96},{96,64},{1,33},{33,1},{65,97},{97,65},{2,34}... | collective-permute-start | bytes 393224 | tf_op jit(solution)/shard_map/ppermute | solution.py:62
  154.6 5.8 %collective-permute-start.34 = (bf16[8,4096]{1,0:T(8,128)(2,1)S(1)}, bf16[8,4096]{1,0:T(8,128)(2,1)S(1)}, u32[]{:S(2)}, u32[]{:S(2)}) collective-permute-start(bf16[8,4096]{1,0:T(8,128)(2,1)S(1)} %fusion.27), channel_id=1, source_target_pairs={{0,8},{16,24},{8,0},{24,16},{1,9},{17,25},{9,1},{25,17},{2,10},{18... | collective-permute-start | bytes 196616 | tf_op jit(solution)/shard_map/ppermute | solution.py:61
  156.8 5.8 %collective-permute-start.40 = (bf16[8,4096]{1,0:T(8,128)(2,1)S(1)}, bf16[8,4096]{1,0:T(8,128)(2,1)S(1)}, u32[]{:S(2)}, u32[]{:S(2)}) collective-permute-start(bf16[8,4096]{1,0:T(8,128)(2,1)S(1)} %fusion.28), channel_id=1, source_target_pairs={{0,64},{32,96},{64,0},{96,32},{1,65},{33,97},{65,1},{97,33},{2,66}... | collective-permute-start | bytes 196616 | tf_op jit(solution)/shard_map/ppermute | solution.py:62
  163.2 5.0 %collective-permute-start.43 = (bf16[2,8192]{1,0:T(2,128)(2,1)S(1)}, bf16[2,8192]{1,0:T(2,128)(2,1)S(1)}, u32[]{:S(2)}, u32[]{:S(2)}) collective-permute-start(bf16[2,8192]{1,0:T(2,128)(2,1)S(1)} %get-tuple-element.68), channel_id=1, source_target_pairs={{0,6},{2,0},{4,2},{6,4},{1,7},{3,1},{5,3},{7,5},{8,14},{10,8},{12,... | collective-permute-start | bytes 98312 | tf_op jit(solution)/shard_map/ppermute | solution.py:26
  166.6 5.1 %collective-permute-start.42 = (bf16[2,8192]{1,0:T(2,128)(2,1)S(1)}, bf16[2,8192]{1,0:T(2,128)(2,1)S(1)}, u32[]{:S(2)}, u32[]{:S(2)}) collective-permute-start(bf16[2,8192]{1,0:T(2,128)(2,1)S(1)} %get-tuple-element.69), channel_id=1, source_target_pairs={{0,2},{2,4},{4,6},{6,0},{1,3},{3,5},{5,7},{7,1},{8,10},{10,12},{12... | collective-permute-start | bytes 98312 | tf_op jit(solution)/shard_map/ppermute | solution.py:26
  166.6 5.5 %collective-permute-start.41 = (bf16[2,8192]{1,0:T(2,128)(2,1)S(1)}, bf16[2,8192]{1,0:T(2,128)(2,1)S(1)}, u32[]{:S(2)}, u32[]{:S(2)}) collective-permute-start(bf16[2,8192]{1,0:T(2,128)(2,1)S(1)} %get-tuple-element.67), channel_id=1, source_target_pairs={{0,4},{2,6},{4,0},{6,2},{1,5},{3,7},{5,1},{7,3},{8,12},{10,14},{12... | collective-permute-start | bytes 98312 | tf_op jit(solution)/shard_map/ppermute | solution.py:26
  168.2 5.3 %copy-start.3 = (bf16[16,8192]{1,0:T(8,128)(2,1)}, bf16[16,8192]{1,0:T(8,128)(2,1)S(1)}, u32[]{:S(2)}) copy-start(bf16[16,8192]{1,0:T(8,128)(2,1)S(1)} %constant_dynamic-update-slice_fusion.2) | copy-start | bytes 786436
